TPU v7x, 32 devices: a whole 2x2x4 slice. The times are simulated.
32 devices in a mesh: shard: 8 (over y, x, core), rep: 4 (over z).
Axes of the slice: x: 2, y: 2, z: 4, core: 2. Of those that a mesh axis runs over, the one named last changes fastest.
Arguments:
- hidden_in: bfloat16 [32, 1024, 1024], P(('shard', 'rep')), may hold values from -6 to 6
- enc_states: bfloat16 [32, 1024, 1024], P(('shard', 'rep')), may hold values from -6 to 6
- cotangent: bfloat16 [32, 1024, 1024], P(('shard', 'rep')), may hold values from -6 to 6
- prefix_len: int32 [32], P(('shard', 'rep')), may hold values from 102 to 512, as said below
- adapter_ids: int32 [32], P(('shard', 'rep')), may hold values from 0 to 7
- self_qkv: bfloat16 [3, 1024, 1024], P(None, 'shard'), may hold values from -0.25 to 0.25
- self_out: bfloat16 [1024, 1024], P('shard'), may hold values from -1.5 to 1.5
- cross_qkv: bfloat16 [3, 1024, 1024], P(None, 'shard'), may hold values from -0.25 to 0.25
- cross_out: bfloat16 [1024, 1024], P('shard'), may hold values from -1.5 to 1.5
- expand_weight: bfloat16 [1024, 4096], P('shard'), may hold values from -0.1875 to 0.1875
- reduce_weight: bfloat16 [4096, 1024], P('shard'), may hold values from -0.125 to 0.125
- attention_adapters: bfloat16 [8, 2, 8, 16, 1024], P(None, None, None, None, 'shard'), may hold values from -0.1875 to 0.1875
- narrow_adapters: bfloat16 [2, 8, 16, 1024], P(None, None, None, 'shard'), may hold values from -0.1875 to 0.1875
- wide_adapters: bfloat16 [2, 8, 16, 4096], P(None, None, None, 'shard'), may hold values from -0.09375 to 0.09375
- norm_gains: float32 [3, 1024], replicated, may hold values from 0.5 to 1.5
- norm_shifts: float32 [3, 1024], replicated, may hold values from -1 to 1
Outputs:
- layer_out: bfloat16 [32, 1024, 1024], P(('shard', 'rep'))
- hidden_grad: float32 [32, 1024, 1024], P(('shard', 'rep'))
- encoder_grad: float32 [32, 1024, 1024], P(('shard', 'rep'))
- attention_grad: float32 [8, 2, 8, 16, 1024], P(None, None, None, None, 'shard')
- narrow_grad: float32 [2, 8, 16, 1024], P(None, None, None, 'shard')
- wide_grad: float32 [2, 8, 16, 4096], P(None, None, None, 'shard')
Inputs may be any that keep to these rules, and one draw needn't show every extreme that they name: `prefix_len`: some sequence has the largest and some the smallest value.
All inputs are finite; a program needn't handle non-finite values.
Results may differ from a plain program's by a relative error of at most 0.03.
The roundings to bfloat16 on the way count: a program that leaves them out, or rounds other values in their place, can miss the bound.
Values may be sent and summed in bfloat16 or wider, within the bound.
No kernel may reach another device: no remote copies, remote signals or barrier semaphores. Data moves between devices by JAX's collectives and lax.ppermute only.
A program may use at most 256 MiB of HBM per device.

v0:
```python
import jax
import jax.numpy as jnp
from jax import lax
from jax.sharding import PartitionSpec as P

HEADS = 16
HEAD_DIM = 64


adapter_scale = 2.0
norm_eps = 1e-05
masked_score = -1000000000.0


def layer_norm(values, gain, shift):
    center = values - jnp.mean(values, axis=-1, keepdims=True)
    variance = jnp.mean(center * center, axis=-1, keepdims=True)
    return center * lax.rsqrt(variance + norm_eps) * gain + shift


def norm_backward(values, gain, shift, upstream):
    result, pullback = jax.vjp(lambda inner: layer_norm(inner, gain, shift), values)
    return pullback(upstream)[0]


def contract_last(left, right):
    return lax.dot_general(
        left, right, (((1,), (1,)), ((), ())), preferred_element_type=jnp.float32
    )


def contract_first(left, right):
    return lax.dot_general(
        left, right, (((0,), (0,)), ((), ())), preferred_element_type=jnp.float32
    )


def project_forward(inputs, weight, down_rows, up_rows):
    reduced = contract_last(inputs, down_rows).astype(jnp.bfloat16)
    output = jnp.dot(inputs, weight, preferred_element_type=jnp.float32)
    output = output + adapter_scale * jnp.dot(reduced, up_rows, preferred_element_type=jnp.float32)
    return (output, reduced)


def projection_backward(upstream, inputs, reduced, weight, down_rows, up_rows):
    reduced_grad = (adapter_scale * contract_last(upstream, up_rows)).astype(jnp.bfloat16)
    input_grad = contract_last(upstream, weight) + jnp.dot(
        reduced_grad, down_rows, preferred_element_type=jnp.float32
    )
    down_grad = contract_first(reduced_grad, inputs)
    up_grad = adapter_scale * contract_first(reduced, upstream)
    return (input_grad, down_grad, up_grad)


def pair_slice(matrix, pair_idx):
    width = 2 * HEAD_DIM
    piece_out = lax.dynamic_slice_in_dim(matrix, pair_idx * width, width, 1)
    return piece_out.reshape(matrix.shape[0], 2, HEAD_DIM)


def pair_scores(query_pair, key_pair, allowed):
    scores = jnp.einsum(
        "qhd,khd->hqk", query_pair, key_pair, preferred_element_type=jnp.float32
    ) * HEAD_DIM ** (-0.5)
    if allowed is not None:
        scores = jnp.where(allowed[None], scores, masked_score)
    return scores


def attend_forward(queries, keys_in, values_in, allowed):
    row_count = queries.shape[0]

    def one_pair(pair_idx, carry):
        mixed, log_total = carry
        scores = pair_scores(pair_slice(queries, pair_idx), pair_slice(keys_in, pair_idx), allowed)
        row_peak = jnp.max(scores, axis=-1, keepdims=True)
        exponent = jnp.exp(scores - row_peak)
        summed = jnp.sum(exponent, axis=-1, keepdims=True)
        probs = (exponent / summed).astype(jnp.bfloat16)
        pair_out = jnp.einsum(
            "hqk,khd->qhd",
            probs,
            pair_slice(values_in, pair_idx),
            preferred_element_type=jnp.float32,
        )
        pair_out = pair_out.reshape(row_count, 2 * HEAD_DIM).astype(jnp.bfloat16)
        mixed = lax.dynamic_update_slice_in_dim(mixed, pair_out, pair_idx * 2 * HEAD_DIM, 1)
        log_total = lax.dynamic_update_slice_in_dim(
            log_total, (row_peak + jnp.log(summed))[..., 0], pair_idx * 2, 0
        )
        return (mixed, log_total)

    initial = (
        jnp.zeros((row_count, HEADS * HEAD_DIM), jnp.bfloat16),
        jnp.zeros((HEADS, row_count), jnp.float32),
    )
    return lax.fori_loop(0, HEADS // 2, one_pair, initial)


def attend_backward(queries, keys_in, values_in, allowed, log_total, mixed_grad):
    row_count = queries.shape[0]
    col_count = keys_in.shape[0]
    score_scale = HEAD_DIM ** (-0.5)

    def one_pair(pair_idx, carry):
        query_grad, key_grad, value_grad = carry
        query_pair = pair_slice(queries, pair_idx)
        key_pair = pair_slice(keys_in, pair_idx)
        value_pair = pair_slice(values_in, pair_idx)
        grad_pair = pair_slice(mixed_grad, pair_idx)
        scores = pair_scores(query_pair, key_pair, allowed)
        lse_pair = lax.dynamic_slice_in_dim(log_total, pair_idx * 2, 2, 0)
        probs = jnp.exp(scores - lse_pair[:, :, None])
        prob_grad = jnp.einsum(
            "qhd,khd->hqk", grad_pair, value_pair, preferred_element_type=jnp.float32
        )
        score_grad = (
            probs * (prob_grad - jnp.sum(prob_grad * probs, axis=-1, keepdims=True))
        ).astype(jnp.bfloat16)
        query_part = (
            jnp.einsum("hqk,khd->qhd", score_grad, key_pair, preferred_element_type=jnp.float32)
            * score_scale
        )
        key_part = (
            jnp.einsum("hqk,qhd->khd", score_grad, query_pair, preferred_element_type=jnp.float32)
            * score_scale
        )
        value_part = jnp.einsum(
            "hqk,qhd->khd",
            probs.astype(jnp.bfloat16),
            grad_pair,
            preferred_element_type=jnp.float32,
        )
        offset = pair_idx * 2 * HEAD_DIM
        query_grad = lax.dynamic_update_slice_in_dim(
            query_grad, query_part.reshape(row_count, 2 * HEAD_DIM), offset, 1
        )
        key_grad = lax.dynamic_update_slice_in_dim(
            key_grad, key_part.reshape(col_count, 2 * HEAD_DIM), offset, 1
        )
        value_grad = lax.dynamic_update_slice_in_dim(
            value_grad, value_part.reshape(col_count, 2 * HEAD_DIM), offset, 1
        )
        return (query_grad, key_grad, value_grad)

    initial = (
        jnp.zeros((row_count, HEADS * HEAD_DIM), jnp.float32),
        jnp.zeros((col_count, HEADS * HEAD_DIM), jnp.float32),
        jnp.zeros((col_count, HEADS * HEAD_DIM), jnp.float32),
    )
    query_grad, key_grad, value_grad = lax.fori_loop(0, HEADS // 2, one_pair, initial)
    return (
        query_grad.astype(jnp.bfloat16),
        key_grad.astype(jnp.bfloat16),
        value_grad.astype(jnp.bfloat16),
    )


def on_device(
    hidden_in,
    enc_states,
    cotangent,
    prefix_len,
    adapter_ids,
    self_qkv,
    self_out,
    cross_qkv,
    cross_out,
    expand_weight,
    reduce_weight,
    attention_adapters,
    narrow_adapters,
    wide_adapters,
    norm_gains,
    norm_shifts,
):
    hidden = hidden_in[0]
    encoder = enc_states[0]
    upstream = cotangent[0].astype(jnp.float32)
    prefix = prefix_len[0]
    adapter_slot = adapter_ids[0]
    seq_count = hidden.shape[0]
    query_pos = lax.broadcasted_iota(jnp.int32, (seq_count, seq_count), 0)
    key_pos = lax.broadcasted_iota(jnp.int32, (seq_count, seq_count), 1)
    allowed = (key_pos <= query_pos) | (key_pos < prefix)
    self_full, self_out_full, self_adapt = (
        lax.all_gather(self_qkv, "shard", axis=1, tiled=True),
        lax.all_gather(self_out, "shard", axis=0, tiled=True),
        lax.all_gather(attention_adapters[:4], "shard", axis=4, tiled=True),
    )
    self_sel = lax.dynamic_index_in_dim(self_adapt, adapter_slot, 2, keepdims=False)
    query_f, query_red = project_forward(hidden, self_full[0], self_sel[0, 0], self_sel[0, 1])
    key_f, key_red = project_forward(hidden, self_full[1], self_sel[1, 0], self_sel[1, 1])
    value_f, value_red = project_forward(hidden, self_full[2], self_sel[2, 0], self_sel[2, 1])
    queries = query_f.astype(jnp.bfloat16)
    keys_in = key_f.astype(jnp.bfloat16)
    values_in = value_f.astype(jnp.bfloat16)
    self_mixed, self_lse = attend_forward(queries, keys_in, values_in, allowed)
    self_branch, self_out_red = project_forward(
        self_mixed, self_out_full, self_sel[3, 0], self_sel[3, 1]
    )
    self_sum = hidden.astype(jnp.float32) + self_branch
    after_self = layer_norm(self_sum, norm_gains[0], norm_shifts[0])
    cross_full, cross_out_full, cross_adapt = (
        lax.all_gather(cross_qkv, "shard", axis=1, tiled=True),
        lax.all_gather(cross_out, "shard", axis=0, tiled=True),
        lax.all_gather(attention_adapters[4:], "shard", axis=4, tiled=True),
    )
    cross_sel = lax.dynamic_index_in_dim(cross_adapt, adapter_slot, 2, keepdims=False)
    cross_in = after_self.astype(jnp.bfloat16)
    cquery_f, cquery_red = project_forward(
        cross_in, cross_full[0], cross_sel[0, 0], cross_sel[0, 1]
    )
    ckey_f, ckey_red = project_forward(encoder, cross_full[1], cross_sel[1, 0], cross_sel[1, 1])
    cvalue_f, cvalue_red = project_forward(encoder, cross_full[2], cross_sel[2, 0], cross_sel[2, 1])
    cross_queries = cquery_f.astype(jnp.bfloat16)
    cross_keys = ckey_f.astype(jnp.bfloat16)
    cross_values = cvalue_f.astype(jnp.bfloat16)
    cross_mixed, cross_lse = attend_forward(cross_queries, cross_keys, cross_values, None)
    cross_branch, cross_out_red = project_forward(
        cross_mixed, cross_out_full, cross_sel[3, 0], cross_sel[3, 1]
    )
    cross_sum = after_self + cross_branch
    after_cross = layer_norm(cross_sum, norm_gains[1], norm_shifts[1])
    expand_full, reduce_full, narrow_full, wide_full = (
        lax.all_gather(expand_weight, "shard", axis=0, tiled=True),
        lax.all_gather(reduce_weight, "shard", axis=0, tiled=True),
        lax.all_gather(narrow_adapters, "shard", axis=3, tiled=True),
        lax.all_gather(wide_adapters, "shard", axis=3, tiled=True),
    )
    narrow_sel = lax.dynamic_index_in_dim(narrow_full, adapter_slot, 1, keepdims=False)
    wide_sel = lax.dynamic_index_in_dim(wide_full, adapter_slot, 1, keepdims=False)
    feed_in = after_cross.astype(jnp.bfloat16)
    expanded, expand_red = project_forward(feed_in, expand_full, narrow_sel[0], wide_sel[0])
    active = jax.nn.gelu(expanded, approximate=False).astype(jnp.bfloat16)
    feed_branch, reduce_red = project_forward(active, reduce_full, wide_sel[1], narrow_sel[1])
    feed_sum = after_cross + feed_branch
    layer_out = layer_norm(feed_sum, norm_gains[2], norm_shifts[2]).astype(jnp.bfloat16)
    expand_reverse, reduce_back, narrow_back, wide_back = (
        lax.all_gather(expand_weight, "shard", axis=0, tiled=True),
        lax.all_gather(reduce_weight, "shard", axis=0, tiled=True),
        lax.all_gather(narrow_adapters, "shard", axis=3, tiled=True),
        lax.all_gather(wide_adapters, "shard", axis=3, tiled=True),
    )
    narrow_bsel = lax.dynamic_index_in_dim(narrow_back, adapter_slot, 1, keepdims=False)
    wide_bsel = lax.dynamic_index_in_dim(wide_back, adapter_slot, 1, keepdims=False)
    grad_feed = norm_backward(feed_sum, norm_gains[2], norm_shifts[2], upstream)
    active_grad, reduce_down_grad, reduce_up_gradient = projection_backward(
        grad_feed.astype(jnp.bfloat16),
        active,
        reduce_red,
        reduce_back,
        wide_bsel[1],
        narrow_bsel[1],
    )
    gelu_result, gelu_pull = jax.vjp(lambda inner: jax.nn.gelu(inner, approximate=False), expanded)
    expanded_grad = gelu_pull(active_grad.astype(jnp.bfloat16).astype(jnp.float32))[0].astype(
        jnp.bfloat16
    )
    feed_in_grad, expand_down_grad, expand_up_grad = projection_backward(
        expanded_grad, feed_in, expand_red, expand_reverse, narrow_bsel[0], wide_bsel[0]
    )
    after_cross_grad = grad_feed + feed_in_grad
    cross_back, cross_out_back, cross_adapt_back = (
        lax.all_gather(cross_qkv, "shard", axis=1, tiled=True),
        lax.all_gather(cross_out, "shard", axis=0, tiled=True),
        lax.all_gather(attention_adapters[4:], "shard", axis=4, tiled=True),
    )
    cross_bsel = lax.dynamic_index_in_dim(cross_adapt_back, adapter_slot, 2, keepdims=False)
    grad_cross = norm_backward(cross_sum, norm_gains[1], norm_shifts[1], after_cross_grad)
    cross_mixed_grad, cout_down, cout_up = projection_backward(
        grad_cross.astype(jnp.bfloat16),
        cross_mixed,
        cross_out_red,
        cross_out_back,
        cross_bsel[3, 0],
        cross_bsel[3, 1],
    )
    cquery_grad, ckey_grad, cvalue_grad = attend_backward(
        cross_queries,
        cross_keys,
        cross_values,
        None,
        cross_lse,
        cross_mixed_grad.astype(jnp.bfloat16),
    )
    cross_in_grad, cquery_down, cquery_up = projection_backward(
        cquery_grad, cross_in, cquery_red, cross_back[0], cross_bsel[0, 0], cross_bsel[0, 1]
    )
    enc_key_grad, ckey_down, ckey_up = projection_backward(
        ckey_grad, encoder, ckey_red, cross_back[1], cross_bsel[1, 0], cross_bsel[1, 1]
    )
    enc_value_grad, cvalue_down, cvalue_up = projection_backward(
        cvalue_grad, encoder, cvalue_red, cross_back[2], cross_bsel[2, 0], cross_bsel[2, 1]
    )
    encoder_grad = enc_key_grad + enc_value_grad
    after_self_grad = grad_cross + cross_in_grad
    self_back, self_out_back, self_adapt_back = (
        lax.all_gather(self_qkv, "shard", axis=1, tiled=True),
        lax.all_gather(self_out, "shard", axis=0, tiled=True),
        lax.all_gather(attention_adapters[:4], "shard", axis=4, tiled=True),
    )
    self_bsel = lax.dynamic_index_in_dim(self_adapt_back, adapter_slot, 2, keepdims=False)
    grad_self = norm_backward(self_sum, norm_gains[0], norm_shifts[0], after_self_grad)
    self_mixed_grad, sout_down, sout_up = projection_backward(
        grad_self.astype(jnp.bfloat16),
        self_mixed,
        self_out_red,
        self_out_back,
        self_bsel[3, 0],
        self_bsel[3, 1],
    )
    query_grad, key_grad, value_grad = attend_backward(
        queries, keys_in, values_in, allowed, self_lse, self_mixed_grad.astype(jnp.bfloat16)
    )
    hid_query, squery_down, squery_up = projection_backward(
        query_grad, hidden, query_red, self_back[0], self_bsel[0, 0], self_bsel[0, 1]
    )
    hidden_key_rows, self_key_down, self_key_up = projection_backward(
        key_grad, hidden, key_red, self_back[1], self_bsel[1, 0], self_bsel[1, 1]
    )
    hid_value, svalue_down, svalue_up = projection_backward(
        value_grad, hidden, value_red, self_back[2], self_bsel[2, 0], self_bsel[2, 1]
    )
    hidden_grad = grad_self + hid_query + hidden_key_rows + hid_value
    attention_parts = (
        (squery_down, squery_up),
        (self_key_down, self_key_up),
        (svalue_down, svalue_up),
        (sout_down, sout_up),
        (cquery_down, cquery_up),
        (ckey_down, ckey_up),
        (cvalue_down, cvalue_up),
        (cout_down, cout_up),
    )
    attention_stack = jnp.stack(
        [jnp.stack([down_part, up_part]) for down_part, up_part in attention_parts]
    )
    narrow_stack = jnp.stack([expand_down_grad, reduce_up_gradient])
    wide_stack = jnp.stack([expand_up_grad, reduce_down_grad])
    adapter_slot_count = attention_adapters.shape[2]
    rank_rows = attention_stack.shape[2]
    attention_fragment = attention_stack.reshape(1, 16, rank_rows, attention_stack.shape[3])
    received = (
        lax.all_to_all(
            attention_fragment.astype(jnp.bfloat16),
            "shard",
            split_axis=3,
            concat_axis=0,
            tiled=True,
        ).astype(attention_fragment.dtype),
        lax.all_to_all(
            narrow_stack[None].astype(jnp.bfloat16),
            "shard",
            split_axis=3,
            concat_axis=0,
            tiled=True,
        ).astype(jnp.float32),
        lax.all_to_all(
            wide_stack[None].astype(jnp.bfloat16), "shard", split_axis=3, concat_axis=0, tiled=True
        ).astype(jnp.float32),
    )
    group_ids = lax.all_gather(adapter_ids, "shard", axis=0, tiled=True)
    one_hot = (
        group_ids[:, None] == jnp.arange(adapter_slot_count, dtype=jnp.int32)[None, :]
    ).astype(jnp.float32)
    selector = one_hot[:, None, :, None, None]
    owned_attention = jnp.sum(selector * received[0][:, :, None], axis=0)
    owned_attention = owned_attention.reshape(
        8, 2, adapter_slot_count, rank_rows, owned_attention.shape[3]
    )
    owned_narrow = jnp.sum(selector * received[1][:, :, None], axis=0)
    owned_wide = jnp.sum(selector * received[2][:, :, None], axis=0)
    attention_grad, narrow_grad, wide_grad = (
        lax.psum(owned_attention.astype(jnp.bfloat16), "rep").astype(jnp.float32),
        lax.psum(owned_narrow.astype(jnp.bfloat16), "rep").astype(jnp.float32),
        lax.psum(owned_wide.astype(jnp.bfloat16), "rep").astype(jnp.float32),
    )
    return (
        layer_out[None],
        hidden_grad[None],
        encoder_grad[None],
        attention_grad,
        narrow_grad,
        wide_grad,
    )


def solution(mesh):
    in_specs = (
        P(("shard", "rep"), None, None),
        P(("shard", "rep"), None, None),
        P(("shard", "rep"), None, None),
        P(("shard", "rep")),
        P(("shard", "rep")),
        P(None, "shard", None),
        P("shard", None),
        P(None, "shard", None),
        P("shard", None),
        P("shard", None),
        P("shard", None),
        P(None, None, None, None, "shard"),
        P(None, None, None, "shard"),
        P(None, None, None, "shard"),
        P(),
        P(),
    )
    out_specs = (
        P(("shard", "rep"), None, None),
        P(("shard", "rep"), None, None),
        P(("shard", "rep"), None, None),
        P(None, None, None, None, "shard"),
        P(None, None, None, "shard"),
        P(None, None, None, "shard"),
    )
    return jax.shard_map(
        on_device, mesh=mesh, in_specs=in_specs, out_specs=out_specs, check_vma=False
    )
```

profile of v0, /device:TPU:0, one launch (start us, length us, event | category | flops | bytes accessed | tf_op | source)
XLA Modules:
  0.0 1214.1 jit_solution(1938074587313677470)
XLA Ops:
  17.8 13.2 %all_gather.50 = bf16[2,8,16,1024]{3,2,1,0:T(8,128)(2,1)} all-gather(bf16[2,8,16,128]{3,2,1,0:T(8,128)(2,1)S(1)} %copy-done.78), channel_id=1, replica_groups=mesh['shard'=8,'rep'=4] {'shard'}, dimensions={3}, use_global_device_ids=true | all-gather | bytes 589824 | tf_op jit(solution)/shard_map/all_gather | solution.py:228
  32.3 7.7 all-reduce
  48.6 24.2 %all-gather.18.cloned.1.call-done = bf16[4,2,8,16,1024]{4,3,2,1,0:T(8,128)(2,1)} async-done(((bf16[4,2,8,16,128]{4,3,2,1,0:T(8,128)(2,1)}), bf16[4,2,8,16,1024]{4,3,2,1,0:T(8,128)(2,1)}) %all-gather.18.cloned.1.call-update) | async-done | bytes 2097168 | tf_op jit(solution)/shard_map/all_gather | solution.py:207
  75.0 45.0 %all-gather.10.cloned.1.call-done = bf16[3,1024,1024]{2,1,0:T(8,128)(2,1)} async-done(((bf16[3,128,1024]{2,1,0:T(8,128)(2,1)}), bf16[3,1024,1024]{2,1,0:T(8,128)(2,1)}) %all-gather.10.cloned.1.call-update) | async-done | bytes 6291472 | tf_op jit(solution)/shard_map/all_gather | solution.py:187
  153.5 130.4 %while.76 = (s32[]{:T(128)}, bf16[1024,1024]{0,1:T(8,128)(2,1)}, f32[16,1024]{1,0:T(8,128)S(1)}, bf16[1024,1024]{0,1:T(8,128)(2,1)}, bf16[1024,1024]{0,1:T(8,128...) while((s32[]{:T(128)}, bf16[1024,1024]{0,1:T(8,128)(2,1)}, ...), condition=%wide.region_3.4_spmd.clone, body=%wide.region_0.3_spmd.clone.sunk | while | flops 564262912 | bytes 66127108 | solution.py:97
  329.8 112.3 %while.74 = (s32[]{:T(128)}, bf16[1024,1024]{0,1:T(8,128)(2,1)}, f32[16,1024]{1,0:T(8,128)S(1)}, bf16[1024,1024]{0,1:T(8,128)(2,1)}, bf16[1024,1024]{0,1:T(8,128...) while((s32[]{:T(128)}, bf16[1024,1024]{0,1:T(8,128)(2,1)}, ...), condition=%wide.region_9.10_spmd, body=%wide.region_6.9_spmd.sunk | while | flops 555874304 | bytes 61931772 | solution.py:97
  456.3 16.1 %fusion.217 = f32[1024,4096]{1,0:T(8,128)} fusion(bf16[1024,1024]{1,0:T(8,128)(2,1)} %copy-done.20, bf16[1024,4096]{1,0:T(8,128)(2,1)} %all-gather.22.cloned.1.call-done), kind=kOutput, calls=%fused_computation.358 | convolution fusion | flops 8589934592 | bytes 27262976 | tf_op jit(solution)/shard_map/dot_general | solution.py:40
  472.3 43.0 %multiply_convert_fusion.2 = (bf16[1024,4096]{1,0:T(8,128)(2,1)}, f32[1024,4096]{1,0:T(8,128)}, f32[1024,4096]{1,0:T(8,128)}) fusion(f32[1024,4096]{1,0:T(8,128)} %fusion.217, bf16[1024,16]{0,1:T(8,128)(2,1)S(1)} %convolution_convert_fusion.8, bf16[2,8,16,4096]{3,2,1,0:T(8,128)(2,1)} %all-gather.24.cloned.1.call-done, s32[]{:T(128)S(6)} %select_n.160), kind=kOutput, calls=%fused_computation.78 | convolution fusion | flops 415236096 | bytes 58884100 | tf_op jit(solution)/shard_map/dot_general | solution.py:41
  515.4 12.9 %fusion.218 = f32[1024,1024]{1,0:T(8,128)S(1)} fusion(bf16[1024,4096]{1,0:T(8,128)(2,1)} %get-tuple-element.1025, bf16[4096,1024]{1,0:T(8,128)(2,1)} %all-gather.26.cloned.1.call-done), kind=kOutput, calls=%fused_computation.359 | convolution fusion | flops 8589934592 | bytes 20971520 | tf_op jit(solution)/shard_map/dot_general | solution.py:40
  543.5 15.0 %fusion.219 = f32[1024,4096]{1,0:T(8,128)} fusion(bf16[1024,1024]{1,0:T(8,128)(2,1)S(1)} %add_convert_fusion.12, bf16[4096,1024]{1,0:T(8,128)(2,1)} %all-gather.26.cloned.1.call-done), kind=kOutput, calls=%fused_computation.360 | convolution fusion | flops 8589934592 | bytes 27262976 | tf_op jit(solution)/shard_map/dot_general | solution.py:27
  558.5 22.3 %fusion.31 = bf16[1024,4096]{1,0:T(8,128)(2,1)} fusion(f32[1024,4096]{1,0:T(8,128)} %get-tuple-element.1026, f32[1024,4096]{1,0:T(8,128)} %get-tuple-element.1058, f32[1024,4096]{1,0:T(8,128)} %fusion.219, bf16[1024,16]{0,1:T(8,128)(2,1)S(1)} %fusion.85, bf16[2,8,16,4096]{3,2,1,0:T(8,128)(2,1)} %all-gather.24.cloned.1.call-done, s32[]{:T(128)S(6)} %add.452, ...), kind=kOutput, calls=%fused_computation.74 | convolution fusion | flops 205520896 | bytes 58884104 | tf_op jit(solution)/shard_map/dot_general | solution.py:47
  580.7 5.4 fusion.41
  590.9 12.9 %fusion.220 = f32[1024,1024]{1,0:T(8,128)} fusion(bf16[1024,4096]{1,0:T(8,128)(2,1)S(1)} %copy-done.12, bf16[1024,4096]{1,0:T(8,128)(2,1)} %all-gather.22.cloned.1.call-done), kind=kOutput, calls=%fused_computation.361 | convolution fusion | flops 8589934592 | bytes 20971520 | tf_op jit(solution)/shard_map/dot_general | solution.py:27
  621.7 182.3 %while.75 = (s32[]{:T(128)}, bf16[1024,1024]{0,1:T(8,128)(2,1)}, bf16[1024,1024]{0,1:T(8,128)(2,1)}, bf16[1024,1024]{0,1:T(8,128)(2,1)}, bf16[1024,1024]{0,1:T(8...) while((s32[]{:T(128)}, bf16[1024,1024]{0,1:T(8,128)(2,1)}, ...), condition=%wide.region_20.21_spmd, body=%wide.region_18.20_spmd.sunk | while | flops 1367865344 | bytes 94953776 | solution.py:151
  827.4 200.7 %while.77 = (s32[]{:T(128)}, bf16[1024,1024]{0,1:T(8,128)(2,1)}, bf16[1024,1024]{0,1:T(8,128)(2,1)}, bf16[1024,1024]{0,1:T(8,128)(2,1)}, bf16[1024,1024]{0,1:T(8...) while((s32[]{:T(128)}, bf16[1024,1024]{0,1:T(8,128)(2,1)}, ...), condition=%wide.region_25.26_spmd.clone, body=%wide.region_23.25_spmd.clone.sunk | while | flops 1376253952 | bytes 99149112 | solution.py:151
  913.2 5.4 multiply_reduce_fusion.16
  938.3 5.4 multiply_reduce_fusion.16
  988.4 5.4 multiply_reduce_fusion.16
  1081.9 6.1 fusion.79
  1101.9 6.5 reshape.484
  1140.8 6.3 convert_bitcast_fusion
  1147.0 5.5 copy.128
  1154.1 11.3 add_bitcast_fusion.1
  1165.4 36.0 %all-reduce.4.cloned.1.call-done = (bf16[8,2,8,16,128]{4,3,2,1,0:T(8,128)(2,1)}, bf16[2,8,16,128]{3,2,1,0:T(8,128)(2,1)}, bf16[2,8,16,512]{3,2,1,0:T(8,128)(2,1)}) async-done(((bf16[8,2,8,16,128]{4,3,2,1,0:T(8,128)(2,1)}, bf16[2,8,16,128]{3,2,1,0:T(8,128)(2,1)}, bf16[2,8,16,512]{3,2,1,0:T(8,128)(2,1)}), (bf16[8,2,8,16,128]{4,3,2,1,0:T(8,128)(2,1)}, bf16[2,8,16,128]{3,2,1,0:T(8,128)(2,1)}, ...) | async-done | bytes 851984 | tf_op jit(solution)/shard_map/psum | solution.py:375
  (836 shorter events, 888.7 us)
Async XLA Ops:
  7.2 66.5 %copy-start = (bf16[1,1024,1024]{2,1,0:T(8,128)(2,1)S(1)}, bf16[1,1024,1024]{2,1,0:T(8,128)(2,1)}, u32[]{:S(2)}) copy-start(bf16[1,1024,1024]{2,1,0:T(8,128)(2,1)} %param.25) | copy-start | bytes 6291460
  7.2 34.9 %all-gather.12.cloned.1.call-start = ((), (), s32[]{:S(2)}) async-start(), calls=%async_computation.4 | async-start | bytes 2359296 | tf_op jit(solution)/shard_map/all_gather | solution.py:189
  9.3 63.4 %all-gather.18.cloned.1.call-start = ((), (), s32[]{:S(2)}) async-start(), calls=%async_computation.7 | async-start | bytes 2359296 | tf_op jit(solution)/shard_map/all_gather | solution.py:207
  10.1 110.0 %all-gather.10.cloned.1.call-start = ((), (), s32[]{:S(2)}) async-start(), calls=%async_computation.3 | async-start | bytes 7077888 | tf_op jit(solution)/shard_map/all_gather | solution.py:187
  10.8 275.1 %all-gather.14.cloned.1.call-start = ((), (), s32[]{:S(2)}) async-start(), calls=%async_computation.5 | async-start | bytes 2359296 | tf_op jit(solution)/shard_map/all_gather | solution.py:188
  11.4 285.9 %all-gather.16.cloned.1.call-start = ((), (), s32[]{:S(2)}) async-start(), calls=%async_computation.6 | async-start | bytes 7077888 | tf_op jit(solution)/shard_map/all_gather | solution.py:205
  12.0 432.7 %all-gather.20.cloned.1.call-start = ((), (), s32[]{:S(2)}) async-start(), calls=%async_computation.8 | async-start | bytes 2359296 | tf_op jit(solution)/shard_map/all_gather | solution.py:206
  12.5 443.7 %all-gather.22.cloned.1.call-start = ((), (), s32[]{:S(2)}) async-start(), calls=%async_computation.9 | async-start | bytes 9437184 | tf_op jit(solution)/shard_map/all_gather | solution.py:226
  13.3 459.0 %all-gather.24.cloned.1.call-start = ((), (), s32[]{:S(2)}) async-start(), calls=%async_computation.10 | async-start | bytes 2359296 | tf_op jit(solution)/shard_map/all_gather | solution.py:229
  14.0 501.3 %all-gather.26.cloned.1.call-start = ((), (), s32[]{:S(2)}) async-start(), calls=%async_computation.11 | async-start | bytes 9437184 | tf_op jit(solution)/shard_map/all_gather | solution.py:227
  43.3 102.7 %copy-start.38 = (bf16[4,2,16,1024]{3,2,1,0:T(8,128)(2,1)}, bf16[4,2,16,1024]{3,2,1,0:T(8,128)(2,1)S(1)}, u32[]{:S(2)}) copy-start(bf16[4,2,16,1024]{3,2,1,0:T(8,128)(2,1)S(1)} %dynamic-slice_bitcast_fusion.1) | copy-start | bytes 786436
  45.6 79.0 %copy-start.46 = (bf16[16,1024]{1,0:T(8,128)(2,1)}, bf16[16,1024]{1,0:T(8,128)(2,1)S(1)}, u32[]{:S(2)}) copy-start(bf16[16,1024]{1,0:T(8,128)(2,1)S(1)} %fusion.104) | copy-start | bytes 98308
  47.9 87.5 %copy-start.50 = (bf16[16,1024]{1,0:T(8,128)(2,1)}, bf16[16,1024]{1,0:T(8,128)(2,1)S(1)}, u32[]{:S(2)}) copy-start(bf16[16,1024]{1,0:T(8,128)(2,1)S(1)} %fusion.107) | copy-start | bytes 98308
  48.6 97.4 %copy-start.48 = (bf16[16,1024]{1,0:T(8,128)(2,1)}, bf16[16,1024]{1,0:T(8,128)(2,1)S(1)}, u32[]{:S(2)}) copy-start(bf16[16,1024]{1,0:T(8,128)(2,1)S(1)} %fusion.110) | copy-start | bytes 98308
  73.7 375.8 %copy-start.36 = (bf16[4,2,16,1024]{3,2,1,0:T(8,128)(2,1)}, bf16[4,2,16,1024]{3,2,1,0:T(8,128)(2,1)S(1)}, u32[]{:S(2)}) copy-start(bf16[4,2,16,1024]{3,2,1,0:T(8,128)(2,1)S(1)} %dynamic-slice_bitcast_fusion) | copy-start | bytes 786436
  74.4 237.4 %copy-start.42 = (bf16[16,1024]{1,0:T(8,128)(2,1)}, bf16[16,1024]{1,0:T(8,128)(2,1)S(1)}, u32[]{:S(2)}) copy-start(bf16[16,1024]{1,0:T(8,128)(2,1)S(1)} %fusion.122) | copy-start | bytes 98308
  75.0 247.1 %copy-start.44 = (bf16[16,1024]{1,0:T(8,128)(2,1)}, bf16[16,1024]{1,0:T(8,128)(2,1)S(1)}, u32[]{:S(2)}) copy-start(bf16[16,1024]{1,0:T(8,128)(2,1)S(1)} %fusion.125) | copy-start | bytes 98308
  292.6 156.9 %copy-start.64 = (f32[1024]{0:T(1024)}, f32[1024]{0:T(1024)S(1)}, u32[]{:S(2)}) copy-start(f32[1024]{0:T(1024)S(1)} %broadcast_multiply_fusion.2) | copy-start | bytes 12292
  293.2 156.3 %copy-start.71 = (f32[1024]{0:T(1024)}, f32[1024]{0:T(1024)S(1)}, u32[]{:S(2)}) copy-start(f32[1024]{0:T(1024)S(1)} %fusion.174) | copy-start | bytes 12292
  827.4 202.9 %copy-start.51 = (bf16[16,1024]{1,0:T(8,128)(2,1)S(1)}, bf16[16,1024]{1,0:T(8,128)(2,1)}, u32[]{:S(2)}) copy-start(bf16[16,1024]{1,0:T(8,128)(2,1)} %copy-done.50) | copy-start | bytes 98308
  1064.6 43.8 %all-to-all-start.1 = ((bf16[8,2,2048]{2,1,0:T(2,128)(2,1)}), bf16[8,2,2048]{2,1,0:T(2,128)(2,1)S(1)}, u32[]{:S(2)}, u32[]{:S(2)}) async-start(bf16[8,2,2048]{2,1,0:T(2,128)(2,1)} %reshape.486), calls=%async_computation.1 | async-start | bytes 131072 | tf_op jit(solution)/shard_map/all_to_all | solution.py:352
  1108.4 11.0 all-to-all-start.2
  1119.4 17.3 %all-to-all-start = ((bf16[8,2,16384]{2,1,0:T(2,128)(2,1)}), bf16[8,2,16384]{2,1,0:T(2,128)(2,1)S(1)}, u32[]{:S(2)}, u32[]{:S(2)}) async-start(bf16[8,2,16384]{2,1,0:T(2,128)(2,1)} %reshape.484), calls=%async_computation | async-start | bytes 1048576 | tf_op jit(solution)/shard_map/all_to_all | solution.py:345
  1122.9 78.5 %all-reduce.4.cloned.1.call-start = ((), (), s32[]{:S(2)}) async-start(), calls=%async_computation.12 | async-start | bytes 1703936 | tf_op jit(solution)/shard_map/psum | solution.py:375
  (134 other events, 671.4 us)
Sparse Core Ops, SparseCore 0:
  10.5 31.6 all-gather.11
  44.6 28.0 all-gather.17
  74.6 45.3 all-gather.9
  121.8 27.7 all-gather.13
  151.4 45.3 all-gather.15
  198.5 27.7 all-gather.19
  228.2 54.3 all-gather.21
  284.5 28.1 all-gather.23
  314.6 54.2 all-gather.25
  1154.2 47.1 all-reduce.3
where the time goes:
time: 1220 us; the launch traced here: 1210 us
  matrix products  632 us (52%)
  local copies, waits for them, and re-layouts  295 us (24%)
  other arithmetic  120 us (10%)
  waiting for transfers between devices  115 us (9%)
  blocking collectives  20.9 us (2%)
  between operations  17.3 us (1%)
    dot_general x32, matrix products, pair_scores(): jnp.einsum('qhd,khd->hqk', query_pair, key_pair, preferred_element_type=j...  99.7 us
    dynamic_slice x112, local copies, waits for them, and re-layouts, pair_slice(): piece_out = lax.dynamic_slice_in_dim(matrix, pair_idx * width, width, 1)  97.2 us
    dot_general x30, matrix products, contract_last(): lax.dot_general(left, right, (((1,), (1,)), ((), ())), preferred_element_...  90.7 us
    dot_general x16, matrix products, one_pair(): jnp.einsum('qhd,khd->hqk', grad_pair, value_pair, preferred_element_type=...  84.6 us
    dot_general x16, matrix products, one_pair(): jnp.einsum('hqk,khd->qhd', probs, pair_slice(values_in, pair_idx), prefer...  81.8 us
    dot_general x10, matrix products, project_forward(): output = jnp.dot(inputs, weight, preferred_element_type=jnp.float32)  64.6 us
    dot_general x10, matrix products, project_forward(): jnp.dot(reduced, up_rows, preferred_element_type=jnp.float32)  61.2 us
    while x96, local copies, waits for them, and re-layouts  54.8 us
  transfers between devices with their start and end apart: 13, of which 5 were waited for; matrix products, arithmetic and copies ran while one was open for 34% of the time, Pallas kernels for 0%

commit v1 on v0

--- a/solution.py
+++ b/solution.py
@@ -1,6 +1,10 @@
+import functools
+
 import jax
 import jax.numpy as jnp
 from jax import lax
+from jax.experimental import pallas as pl
+from jax.experimental.pallas import tpu as pltpu
 from jax.sharding import PartitionSpec as P
 
 HEADS = 16
@@ -52,108 +56,96 @@
     return (input_grad, down_grad, up_grad)
 
 
-def pair_slice(matrix, pair_idx):
-    width = 2 * HEAD_DIM
-    piece_out = lax.dynamic_slice_in_dim(matrix, pair_idx * width, width, 1)
-    return piece_out.reshape(matrix.shape[0], 2, HEAD_DIM)
-
-
-def pair_scores(query_pair, key_pair, allowed):
-    scores = jnp.einsum(
-        "qhd,khd->hqk", query_pair, key_pair, preferred_element_type=jnp.float32
-    ) * HEAD_DIM ** (-0.5)
-    if allowed is not None:
-        scores = jnp.where(allowed[None], scores, masked_score)
-    return scores
-
-
-def attend_forward(queries, keys_in, values_in, allowed):
-    row_count = queries.shape[0]
-
-    def one_pair(pair_idx, carry):
-        mixed, log_total = carry
-        scores = pair_scores(pair_slice(queries, pair_idx), pair_slice(keys_in, pair_idx), allowed)
-        row_peak = jnp.max(scores, axis=-1, keepdims=True)
-        exponent = jnp.exp(scores - row_peak)
-        summed = jnp.sum(exponent, axis=-1, keepdims=True)
-        probs = (exponent / summed).astype(jnp.bfloat16)
-        pair_out = jnp.einsum(
-            "hqk,khd->qhd",
-            probs,
-            pair_slice(values_in, pair_idx),
-            preferred_element_type=jnp.float32,
-        )
-        pair_out = pair_out.reshape(row_count, 2 * HEAD_DIM).astype(jnp.bfloat16)
-        mixed = lax.dynamic_update_slice_in_dim(mixed, pair_out, pair_idx * 2 * HEAD_DIM, 1)
-        log_total = lax.dynamic_update_slice_in_dim(
-            log_total, (row_peak + jnp.log(summed))[..., 0], pair_idx * 2, 0
-        )
-        return (mixed, log_total)
-
-    initial = (
-        jnp.zeros((row_count, HEADS * HEAD_DIM), jnp.bfloat16),
-        jnp.zeros((HEADS, row_count), jnp.float32),
-    )
-    return lax.fori_loop(0, HEADS // 2, one_pair, initial)
-
-
-def attend_backward(queries, keys_in, values_in, allowed, log_total, mixed_grad):
-    row_count = queries.shape[0]
-    col_count = keys_in.shape[0]
-    score_scale = HEAD_DIM ** (-0.5)
-
-    def one_pair(pair_idx, carry):
-        query_grad, key_grad, value_grad = carry
-        query_pair = pair_slice(queries, pair_idx)
-        key_pair = pair_slice(keys_in, pair_idx)
-        value_pair = pair_slice(values_in, pair_idx)
-        grad_pair = pair_slice(mixed_grad, pair_idx)
-        scores = pair_scores(query_pair, key_pair, allowed)
-        lse_pair = lax.dynamic_slice_in_dim(log_total, pair_idx * 2, 2, 0)
-        probs = jnp.exp(scores - lse_pair[:, :, None])
-        prob_grad = jnp.einsum(
-            "qhd,khd->hqk", grad_pair, value_pair, preferred_element_type=jnp.float32
-        )
-        score_grad = (
-            probs * (prob_grad - jnp.sum(prob_grad * probs, axis=-1, keepdims=True))
-        ).astype(jnp.bfloat16)
-        query_part = (
-            jnp.einsum("hqk,khd->qhd", score_grad, key_pair, preferred_element_type=jnp.float32)
-            * score_scale
-        )
-        key_part = (
-            jnp.einsum("hqk,qhd->khd", score_grad, query_pair, preferred_element_type=jnp.float32)
-            * score_scale
-        )
-        value_part = jnp.einsum(
-            "hqk,qhd->khd",
-            probs.astype(jnp.bfloat16),
-            grad_pair,
-            preferred_element_type=jnp.float32,
-        )
-        offset = pair_idx * 2 * HEAD_DIM
-        query_grad = lax.dynamic_update_slice_in_dim(
-            query_grad, query_part.reshape(row_count, 2 * HEAD_DIM), offset, 1
-        )
-        key_grad = lax.dynamic_update_slice_in_dim(
-            key_grad, key_part.reshape(col_count, 2 * HEAD_DIM), offset, 1
-        )
-        value_grad = lax.dynamic_update_slice_in_dim(
-            value_grad, value_part.reshape(col_count, 2 * HEAD_DIM), offset, 1
-        )
-        return (query_grad, key_grad, value_grad)
-
-    initial = (
-        jnp.zeros((row_count, HEADS * HEAD_DIM), jnp.float32),
-        jnp.zeros((col_count, HEADS * HEAD_DIM), jnp.float32),
-        jnp.zeros((col_count, HEADS * HEAD_DIM), jnp.float32),
-    )
-    query_grad, key_grad, value_grad = lax.fori_loop(0, HEADS // 2, one_pair, initial)
-    return (
-        query_grad.astype(jnp.bfloat16),
-        key_grad.astype(jnp.bfloat16),
-        value_grad.astype(jnp.bfloat16),
-    )
+def dg(left, right, left_dim, right_dim):
+    return lax.dot_general(
+        left, right, (((left_dim,), (right_dim,)), ((), ())), preferred_element_type=jnp.float32
+    )
+
+
+def spans(tq, masked, maxp=512):
+    out=[]
+    for i in range(1024//tq):
+        lo=i*tq
+        hi=max(lo+tq,maxp) if masked else 1024
+        out.append((lo,hi))
+    return out
+def mask_scores(s, lo, tq, hi, prefix):
+    if lo==0: keep,rest=None,s
+    else: keep,rest=s[:,:lo],s[:,lo:]
+    w=hi-lo
+    kp=lax.broadcasted_iota(jnp.int32,(tq,w),1)+lo
+    qp=lax.broadcasted_iota(jnp.int32,(tq,w),0)+lo
+    rest=jnp.where((kp<=qp)|(kp<prefix),rest,masked_score)
+    return rest if keep is None else jnp.concatenate([keep,rest],axis=1)
+def fwd_kernel(prefix_ref,q_ref,k_ref,v_ref,o_ref,lse_ref,*,masked,tq):
+    prefix=prefix_ref[0] if masked else None
+    lane=lax.broadcasted_iota(jnp.int32,(1,128),1)
+    k=k_ref[...]; v=v_ref[...]
+    for lo,hi in spans(tq,masked):
+        q=q_ref[lo:lo+tq,:]*jnp.asarray(0.125,jnp.bfloat16)
+        outs=[]
+        for h in range(2):
+            sel=(lane<64) if h==0 else (lane>=64)
+            qh=jnp.where(sel,q,jnp.zeros_like(q))
+            s=dg(qh,k[:hi],1,1)
+            if masked: s=mask_scores(s,lo,tq,hi,prefix)
+            m=jnp.max(s,axis=-1,keepdims=True)
+            e=jnp.exp(s-m)
+            l=jnp.sum(e,axis=-1,keepdims=True)
+            o=dg(e.astype(jnp.bfloat16),v[:hi],1,0)*(1.0/l)
+            outs.append(o)
+            lse_ref[0,lo:lo+tq,h:h+1]=m+jnp.log(l)
+        o_ref[lo:lo+tq,:]=jnp.where(lane<64,outs[0],outs[1]).astype(jnp.bfloat16)
+def attn_fwd(q,k,v,prefix,masked,tq=256,pick=(0,0,0)):
+    spec=lambda off: pl.BlockSpec((1024,128),lambda i:(0,i+off))
+    return pl.pallas_call(functools.partial(fwd_kernel,masked=masked,tq=tq),grid=(8,),
+        in_specs=[pl.BlockSpec(memory_space=pltpu.SMEM),spec(pick[0]),spec(pick[1]),spec(pick[2])],
+        out_specs=[spec(0),pl.BlockSpec((1,1024,2),lambda i:(i,0,0))],
+        out_shape=[jax.ShapeDtypeStruct((1024,1024),jnp.bfloat16),jax.ShapeDtypeStruct((8,1024,2),jnp.float32)],
+        name="attn_fwd_%s_%d"%("m" if masked else "f",tq))(prefix,q,k,v)
+def bwd_kernel(prefix_ref,q_ref,k_ref,v_ref,do_ref,lse_ref,dq_ref,dk_ref,dv_ref,dkt,dvt,*,masked,tq,mode):
+    prefix=prefix_ref[0] if masked else None
+    lane=lax.broadcasted_iota(jnp.int32,(1,128),1)
+    k=k_ref[...]; v=v_ref[...]
+    dkt[...]=jnp.zeros_like(dkt); dvt[...]=jnp.zeros_like(dvt)
+    for lo,hi in spans(tq,masked):
+        q=q_ref[lo:lo+tq,:]*jnp.asarray(0.125,jnp.bfloat16)
+        do=do_ref[lo:lo+tq,:]
+        if mode=="wt":
+            qt=q.T; dot=do.T
+        dqs=[]
+        for h in range(2):
+            sel=(lane<64) if h==0 else (lane>=64)
+            qh=jnp.where(sel,q,jnp.zeros_like(q)); doh=jnp.where(sel,do,jnp.zeros_like(do))
+            s=dg(qh,k[:hi],1,1)
+            if masked: s=mask_scores(s,lo,tq,hi,prefix)
+            p=jnp.exp(s-lse_ref[0,lo:lo+tq,h:h+1])
+            dp=dg(doh,v[:hi],1,1)
+            d=jnp.sum(p*dp,axis=-1,keepdims=True)
+            ds=(p*(dp-d)).astype(jnp.bfloat16)
+            pb=p.astype(jnp.bfloat16)
+            dqs.append(dg(ds,k[:hi],1,0))
+            if mode=="wt":
+                r=slice(64*h,64*h+64)
+                dvt[r,:hi]+=dg(dot[r],pb,1,0)
+                dkt[r,:hi]+=dg(qt[r],ds,1,0)
+            else:
+                dvt[:hi]+=dg(pb,doh,0,0)
+                dkt[:hi]+=dg(ds,qh,0,0)
+        dq_ref[lo:lo+tq,:]=(jnp.where(lane<64,dqs[0],dqs[1])*0.125).astype(jnp.bfloat16)
+    if mode=="wt":
+        dk_ref[...]=dkt[...].T.astype(jnp.bfloat16); dv_ref[...]=dvt[...].T.astype(jnp.bfloat16)
+    else:
+        dk_ref[...]=dkt[...].astype(jnp.bfloat16); dv_ref[...]=dvt[...].astype(jnp.bfloat16)
+def attn_bwd(q,k,v,do,lse,prefix,masked,tq=256,pick=(0,0,0),mode="wt"):
+    spec=lambda off: pl.BlockSpec((1024,128),lambda i:(0,i+off))
+    acc=(128,1024) if mode=="wt" else (1024,128)
+    return pl.pallas_call(functools.partial(bwd_kernel,masked=masked,tq=tq,mode=mode),grid=(8,),
+        in_specs=[pl.BlockSpec(memory_space=pltpu.SMEM),spec(pick[0]),spec(pick[1]),spec(pick[2]),spec(0),pl.BlockSpec((1,1024,2),lambda i:(i,0,0))],
+        out_specs=[spec(0)]*3,
+        out_shape=[jax.ShapeDtypeStruct((1024,1024),jnp.bfloat16)]*3,
+        scratch_shapes=[pltpu.VMEM(acc,jnp.float32)]*2,
+        name="attn_bwd_%s_%d_%s"%("m" if masked else "f",tq,mode))(prefix,q,k,v,do,lse)
 
 
 def on_device(
@@ -177,12 +169,7 @@
     hidden = hidden_in[0]
     encoder = enc_states[0]
     upstream = cotangent[0].astype(jnp.float32)
-    prefix = prefix_len[0]
     adapter_slot = adapter_ids[0]
-    seq_count = hidden.shape[0]
-    query_pos = lax.broadcasted_iota(jnp.int32, (seq_count, seq_count), 0)
-    key_pos = lax.broadcasted_iota(jnp.int32, (seq_count, seq_count), 1)
-    allowed = (key_pos <= query_pos) | (key_pos < prefix)
     self_full, self_out_full, self_adapt = (
         lax.all_gather(self_qkv, "shard", axis=1, tiled=True),
         lax.all_gather(self_out, "shard", axis=0, tiled=True),
@@ -195,7 +182,7 @@
     queries = query_f.astype(jnp.bfloat16)
     keys_in = key_f.astype(jnp.bfloat16)
     values_in = value_f.astype(jnp.bfloat16)
-    self_mixed, self_lse = attend_forward(queries, keys_in, values_in, allowed)
+    self_mixed, self_lse = attn_fwd(queries, keys_in, values_in, prefix_len, True)
     self_branch, self_out_red = project_forward(
         self_mixed, self_out_full, self_sel[3, 0], self_sel[3, 1]
     )
@@ -216,7 +203,9 @@
     cross_queries = cquery_f.astype(jnp.bfloat16)
     cross_keys = ckey_f.astype(jnp.bfloat16)
     cross_values = cvalue_f.astype(jnp.bfloat16)
-    cross_mixed, cross_lse = attend_forward(cross_queries, cross_keys, cross_values, None)
+    cross_mixed, cross_lse = attn_fwd(
+        cross_queries, cross_keys, cross_values, prefix_len, False
+    )
     cross_branch, cross_out_red = project_forward(
         cross_mixed, cross_out_full, cross_sel[3, 0], cross_sel[3, 1]
     )
@@ -232,7 +221,9 @@
     wide_sel = lax.dynamic_index_in_dim(wide_full, adapter_slot, 1, keepdims=False)
     feed_in = after_cross.astype(jnp.bfloat16)
     expanded, expand_red = project_forward(feed_in, expand_full, narrow_sel[0], wide_sel[0])
-    active = jax.nn.gelu(expanded, approximate=False).astype(jnp.bfloat16)
+    cdf = 0.5 + 0.5 * lax.erf(expanded * 0.7071067811865476)
+    active = (expanded * cdf).astype(jnp.bfloat16)
+    slope = cdf + expanded * jnp.exp(-0.5 * expanded * expanded) * 0.3989422804014327
     feed_branch, reduce_red = project_forward(active, reduce_full, wide_sel[1], narrow_sel[1])
     feed_sum = after_cross + feed_branch
     layer_out = layer_norm(feed_sum, norm_gains[2], norm_shifts[2]).astype(jnp.bfloat16)
@@ -253,8 +244,7 @@
         wide_bsel[1],
         narrow_bsel[1],
     )
-    gelu_result, gelu_pull = jax.vjp(lambda inner: jax.nn.gelu(inner, approximate=False), expanded)
-    expanded_grad = gelu_pull(active_grad.astype(jnp.bfloat16).astype(jnp.float32))[0].astype(
+    expanded_grad = (active_grad.astype(jnp.bfloat16).astype(jnp.float32) * slope).astype(
         jnp.bfloat16
     )
     feed_in_grad, expand_down_grad, expand_up_grad = projection_backward(
@@ -276,13 +266,14 @@
         cross_bsel[3, 0],
         cross_bsel[3, 1],
     )
-    cquery_grad, ckey_grad, cvalue_grad = attend_backward(
+    cquery_grad, ckey_grad, cvalue_grad = attn_bwd(
         cross_queries,
         cross_keys,
         cross_values,
-        None,
+        cross_mixed_grad.astype(jnp.bfloat16),
         cross_lse,
-        cross_mixed_grad.astype(jnp.bfloat16),
+        prefix_len,
+        False,
     )
     cross_in_grad, cquery_down, cquery_up = projection_backward(
         cquery_grad, cross_in, cquery_red, cross_back[0], cross_bsel[0, 0], cross_bsel[0, 1]
@@ -310,8 +301,14 @@
         self_bsel[3, 0],
         self_bsel[3, 1],
     )
-    query_grad, key_grad, value_grad = attend_backward(
-        queries, keys_in, values_in, allowed, self_lse, self_mixed_grad.astype(jnp.bfloat16)
+    query_grad, key_grad, value_grad = attn_bwd(
+        queries,
+        keys_in,
+        values_in,
+        self_mixed_grad.astype(jnp.bfloat16),
+        self_lse,
+        prefix_len,
+        True,
     )
     hid_query, squery_down, squery_up = projection_backward(
         query_grad, hidden, query_red, self_back[0], self_bsel[0, 0], self_bsel[0, 1]

time: 1220 us -> 776 us (0.64)
  matrix products: 632 us -> 242 us
  local copies, waits for them, and re-layouts: 295 us -> 58.3 us
  Pallas kernels: 0 us -> 167 us
  waiting for transfers between devices: 115 us -> 211 us
  other arithmetic: 120 us -> 38.6 us
    dot_general x112 -> x0, matrix products: 335 us -> none  [the longest x32 99.7 us: pair_scores(): jnp.einsum('qhd,khd->hqk', query_pair, key_pair, preferred_element_type=j...]
    pallas_call x0 -> x4, Pallas kernels: none -> 167 us  [the longest x2 103 us: attn_bwd(): pl.pallas_call(functools.partial(bwd_kernel, masked=masked, tq=tq, mode=m...]
    dynamic_slice x128 -> x0, local copies, waits for them, and re-layouts: 111 us -> none  [the longest x112 97.2 us: pair_slice(): piece_out = lax.dynamic_slice_in_dim(matrix, pair_idx * width, width, 1)]
    while x99 -> x0, local copies, waits for them, and re-layouts: 67.1 us -> none
    convert_element_type x16 -> x0, other arithmetic: 41.6 us -> none  [one_pair(): score_grad = (probs * (prob_grad - jnp.sum(prob_grad * probs, axis=-1, ke...]
    all_gather x1, waiting for transfers between devices: 0.02 us -> 39.7 us  [on_device(): lax.all_gather(reduce_weight, 'shard', axis=0, tiled=True)]
    dynamic_update_slice x48 -> x0, local copies, waits for them, and re-layouts: 37.1 us -> none  [the longest x16 13.7 us: one_pair(): lax.dynamic_update_slice_in_dim(value_grad, value_part.reshape(col_count,...]
    dot_general x10, matrix products: 61.2 us -> 33.1 us  [project_forward(): jnp.dot(reduced, up_rows, preferred_element_type=jnp.float32)]
  transfers between devices with their start and end apart: 13 -> 13, of which waited for: 5 -> 9; matrix products, arithmetic and copies ran while one was open for 34% -> 22% of each run, Pallas kernels for 0% -> 8%
where the time goes in v1:
time: 776 us; the launch traced here: 766 us
  matrix products  242 us (31%)
  waiting for transfers between devices  211 us (27%)
  Pallas kernels  167 us (22%)
  local copies, waits for them, and re-layouts  58.3 us (8%)
  other arithmetic  38.6 us (5%)
  blocking collectives  20.1 us (3%)
  between operations  17 us (2%)
  starting transfers between devices  11.6 us (1%)
    pallas_call x2, Pallas kernels, attn_bwd(): pl.pallas_call(functools.partial(bwd_kernel, masked=masked, tq=tq, mode=m...  103 us
    dot_general x30, matrix products, contract_last(): lax.dot_general(left, right, (((1,), (1,)), ((), ())), preferred_element_...  86 us
    pallas_call x2, Pallas kernels, attn_fwd(): pl.pallas_call(functools.partial(fwd_kernel, masked=masked, tq=tq), grid=...  64.4 us
    dot_general x10, matrix products, project_forward(): output = jnp.dot(inputs, weight, preferred_element_type=jnp.float32)  56.9 us
    all_gather x1, waiting for transfers between devices, on_device(): lax.all_gather(self_qkv, 'shard', axis=1, tiled=True)  45 us
    dot_general x10, matrix products, projection_backward(): jnp.dot(reduced_grad, down_rows, preferred_element_type=jnp.float32)  44.8 us
    all_gather x1, waiting for transfers between devices, on_device(): lax.all_gather(reduce_weight, 'shard', axis=0, tiled=True)  39.7 us
    psum x1, waiting for transfers between devices, on_device(): lax.psum(owned_attention.astype(jnp.bfloat16), 'rep').astype(jnp.float32)  36.1 us
  transfers between devices with their start and end apart: 13, of which 9 were waited for; matrix products, arithmetic and copies ran while one was open for 22% of the time, Pallas kernels for 8%

profile of v1, /device:TPU:0, one launch (start us, length us, event | category | flops | bytes accessed | tf_op | source)
XLA Modules:
  0.0 766.1 jit_solution(5251023143612237706)
XLA Ops:
  16.1 12.9 %all_gather.50 = bf16[2,8,16,1024]{3,2,1,0:T(8,128)(2,1)S(1)} all-gather(bf16[2,8,16,128]{3,2,1,0:T(8,128)(2,1)S(1)} %copy-done.71), channel_id=1, replica_groups=mesh['shard'=8,'rep'=4] {'shard'}, dimensions={3}, use_global_device_ids=true | all-gather | bytes 589824 | tf_op jit(solution)/shard_map/all_gather | solution.py:217
  30.4 7.2 all-reduce
  49.2 24.2 %all-gather.18.cloned.1.call-done = bf16[4,2,8,16,1024]{4,3,2,1,0:T(8,128)(2,1)} async-done(((bf16[4,2,8,16,128]{4,3,2,1,0:T(8,128)(2,1)}), bf16[4,2,8,16,1024]{4,3,2,1,0:T(8,128)(2,1)}) %all-gather.18.cloned.1.call-update) | async-done | bytes 2097168 | tf_op jit(solution)/shard_map/all_gather | solution.py:194
  75.7 45.0 %all-gather.10.cloned.1.call-done = bf16[3,1024,1024]{2,1,0:T(8,128)(2,1)} async-done(((bf16[3,128,1024]{2,1,0:T(8,128)(2,1)}), bf16[3,1024,1024]{2,1,0:T(8,128)(2,1)}) %all-gather.10.cloned.1.call-update) | async-done | bytes 6291472 | tf_op jit(solution)/shard_map/all_gather | solution.py:174
  136.5 29.1 %attn_fwd_m_256.1 = (bf16[1024,1024]{1,0:T(8,128)(2,1)}, f32[8,1024,2]{2,1,0:T(8,128)}) custom-call(s32[1]{0:T(128)S(6)} %copy.88.prefix_ref, bf16[1024,1024]{1,0:T(8,128)(2,1)} %add_convert_fusion.9.q_ref, bf16[1024,1024]{1,0:T(8,128)(2,1)} %add_convert_fusion.8.k_ref, bf16[1024,1024]{1,0:T(8,128)(2,1)} %add_convert_fusion.7.v_ref), custom_call_target="tpu_custom_call" | custom-call | tf_op jit(solution)/shard_map/attn_fwd_m_256/pallas_call | solution.py:101
  178.3 19.1 %all-gather.16.cloned.1.call-done = bf16[3,1024,1024]{2,1,0:T(8,128)(2,1)} async-done(((bf16[3,128,1024]{2,1,0:T(8,128)(2,1)}), bf16[3,1024,1024]{2,1,0:T(8,128)(2,1)}) %all-gather.16.cloned.1.call-update) | async-done | bytes 6291472 | tf_op jit(solution)/shard_map/all_gather | solution.py:192
  214.4 35.3 %attn_fwd_f_256.1 = (bf16[1024,1024]{1,0:T(8,128)(2,1)}, f32[8,1024,2]{2,1,0:T(8,128)}) custom-call(s32[1]{0:T(128)S(6)} %copy.88.prefix_ref, bf16[1024,1024]{1,0:T(8,128)(2,1)} %add_convert_fusion.6.q_ref, bf16[1024,1024]{1,0:T(8,128)(2,1)} %add_convert_fusion.5.k_ref, bf16[1024,1024]{1,0:T(8,128)(2,1)} %add_convert_fusion.4.v_ref), custom_call_target="tpu_custom_call" | custom-call | tf_op jit(solution)/shard_map/attn_fwd_f_256/pallas_call | solution.py:101
  262.5 20.7 %all-gather.22.cloned.1.call-done = bf16[1024,4096]{1,0:T(8,128)(2,1)} async-done(((bf16[128,4096]{1,0:T(8,128)(2,1)}), bf16[1024,4096]{1,0:T(8,128)(2,1)}) %all-gather.22.cloned.1.call-update) | async-done | bytes 8388624 | tf_op jit(solution)/shard_map/all_gather | solution.py:215
  283.2 16.2 %fusion.163 = f32[1024,4096]{1,0:T(8,128)} fusion(bf16[1024,1024]{1,0:T(8,128)(2,1)} %copy-done.16, bf16[1024,4096]{1,0:T(8,128)(2,1)} %all-gather.22.cloned.1.call-done), kind=kOutput, calls=%fused_computation.255 | convolution fusion | flops 8589934592 | bytes 27262976 | tf_op jit(solution)/shard_map/dot_general | solution.py:44
  299.4 13.8 %all-gather.24.cloned.1.call-done = bf16[2,8,16,4096]{3,2,1,0:T(8,128)(2,1)} async-done(((bf16[2,8,16,512]{3,2,1,0:T(8,128)(2,1)}), bf16[2,8,16,4096]{3,2,1,0:T(8,128)(2,1)}) %all-gather.24.cloned.1.call-update) | async-done | bytes 2097168 | tf_op jit(solution)/shard_map/all_gather | solution.py:218
  313.2 16.5 %multiply_convert_fusion = (bf16[1024,4096]{1,0:T(8,128)(2,1)}, f32[1024,4096]{1,0:T(8,128)}) fusion(f32[1024,4096]{1,0:T(8,128)} %fusion.163, bf16[1024,16]{0,1:T(8,128)(2,1)S(1)} %convolution_convert_fusion.6, bf16[2,8,16,4096]{3,2,1,0:T(8,128)(2,1)} %all-gather.24.cloned.1.call-done, s32[]{:T(128)S(6)} %select_n.13), kind=kOutput, calls=%fused_computation.8 | convolution fusion | flops 163577856 | bytes 42106884 | tf_op jit(solution)/shard_map/dot_general | solution.py:45
  329.7 39.7 %all-gather.26.cloned.1.call-done = bf16[4096,1024]{1,0:T(8,128)(2,1)} async-done(((bf16[512,1024]{1,0:T(8,128)(2,1)}), bf16[4096,1024]{1,0:T(8,128)(2,1)}) %all-gather.26.cloned.1.call-update) | async-done | bytes 8388624 | tf_op jit(solution)/shard_map/all_gather | solution.py:216
  369.4 12.7 %fusion.164 = f32[1024,1024]{1,0:T(8,128)S(1)} fusion(bf16[1024,4096]{1,0:T(8,128)(2,1)} %get-tuple-element.52, bf16[4096,1024]{1,0:T(8,128)(2,1)} %all-gather.26.cloned.1.call-done), kind=kOutput, calls=%fused_computation.256 | convolution fusion | flops 8589934592 | bytes 20971520 | tf_op jit(solution)/shard_map/dot_general | solution.py:44
  395.1 14.6 %fusion.165 = f32[1024,4096]{1,0:T(8,128)} fusion(bf16[1024,1024]{1,0:T(8,128)(2,1)S(1)} %add_convert_fusion.12, bf16[4096,1024]{1,0:T(8,128)(2,1)} %all-gather.26.cloned.1.call-done), kind=kOutput, calls=%fused_computation.257 | convolution fusion | flops 8589934592 | bytes 27262976 | tf_op jit(solution)/shard_map/dot_general | solution.py:31
  409.6 15.1 %fusion.5 = bf16[1024,4096]{1,0:T(8,128)(2,1)S(1)} fusion(f32[1024,4096]{1,0:T(8,128)} %get-tuple-element.53, f32[1024,4096]{1,0:T(8,128)} %fusion.165, bf16[1024,16]{0,1:T(8,128)(2,1)S(1)} %fusion.52, bf16[2,8,16,4096]{3,2,1,0:T(8,128)(2,1)} %all-gather.24.cloned.1.call-done, s32[]{:T(128)S(6)} %add.221, s32[]{:T(128)S(6)} %select_n.13), kind=kOutput, calls=%fused_computation.6 | convolution fusion | flops 188743680 | bytes 42106888 | tf_op jit(solution)/shard_map/dot_general | solution.py:51
  429.7 11.4 %fusion.166 = f32[1024,1024]{1,0:T(8,128)S(1)} fusion(bf16[1024,4096]{1,0:T(8,128)(2,1)S(1)} %fusion.5, bf16[1024,4096]{1,0:T(8,128)(2,1)} %all-gather.22.cloned.1.call-done), kind=kOutput, calls=%fused_computation.258 | convolution fusion | flops 8589934592 | bytes 20971520 | tf_op jit(solution)/shard_map/dot_general | solution.py:31
  452.6 58.1 %attn_bwd_f_256_wt.1 = (bf16[1024,1024]{1,0:T(8,128)(2,1)}, bf16[1024,1024]{1,0:T(8,128)(2,1)}, bf16[1024,1024]{1,0:T(8,128)(2,1)}) custom-call(s32[1]{0:T(128)S(6)} %copy.88.prefix_ref, bf16[1024,1024]{1,0:T(8,128)(2,1)} %add_convert_fusion.6.q_ref, bf16[1024,1024]{1,0:T(8,128)(2,1)} %add_convert_fusion.5.k_ref, ...), custom_call_target="tpu_custom_call" | custom-call | tf_op jit(solution)/shard_map/attn_bwd_f_256_wt/pallas_call | solution.py:143
  529.1 44.8 %attn_bwd_m_256_wt.1 = (bf16[1024,1024]{1,0:T(8,128)(2,1)}, bf16[1024,1024]{1,0:T(8,128)(2,1)}, bf16[1024,1024]{1,0:T(8,128)(2,1)}) custom-call(s32[1]{0:T(128)S(6)} %copy.88.prefix_ref, bf16[1024,1024]{1,0:T(8,128)(2,1)} %add_convert_fusion.9.q_ref, bf16[1024,1024]{1,0:T(8,128)(2,1)} %add_convert_fusion.8.k_ref, ...), custom_call_target="tpu_custom_call" | custom-call | tf_op jit(solution)/shard_map/attn_bwd_m_256_wt/pallas_call | solution.py:143
  652.5 6.7 reshape.238
  682.3 5.1 copy.66
  692.7 6.3 convert_bitcast_fusion
  699.0 5.5 copy.62
  706.0 11.2 %add_bitcast_fusion.1 = f32[1,1024,1024]{2,1,0:T(8,128)} fusion(f32[1024,1024]{1,0:T(8,128)} %fusion.47, f32[1024,1024]{1,0:T(8,128)} %fusion.46, f32[1024,1024]{1,0:T(8,128)} %fusion.138, f32[1024,1024]{1,0:T(8,128)} %fusion.45, f32[1024,1024]{1,0:T(8,128)} %fusion.137, f32[1024,1024]{1,0:T(8,128)} %copy-done.13, bf16[1024,16]{0,1:T(8,128)(2,1)S(1)} %copy-done.58, ...), kind=kOutput, calls=%fused_computation.28 | convolution fusion | flops 40894464 | bytes 29429760 | tf_op jit(solution)/shard_map/dot_general | solution.py:51
  717.2 36.1 %all-reduce.4.cloned.1.call-done = (bf16[8,2,8,16,128]{4,3,2,1,0:T(8,128)(2,1)}, bf16[2,8,16,128]{3,2,1,0:T(8,128)(2,1)}, bf16[2,8,16,512]{3,2,1,0:T(8,128)(2,1)}) async-done(((bf16[8,2,8,16,128]{4,3,2,1,0:T(8,128)(2,1)}, bf16[2,8,16,128]{3,2,1,0:T(8,128)(2,1)}, bf16[2,8,16,512]{3,2,1,0:T(8,128)(2,1)}), (bf16[8,2,8,16,128]{4,3,2,1,0:T(8,128)(2,1)}, bf16[2,8,16,128]{3,2,1,0:T(8,128)(2,1)}, ...) | async-done | bytes 851984 | tf_op jit(solution)/shard_map/psum | solution.py:372
  (331 shorter events, 241.7 us)
Async XLA Ops:
  7.2 35.6 %all-gather.12.cloned.1.call-start = ((), (), s32[]{:S(2)}) async-start(), calls=%async_computation.4 | async-start | bytes 2359296 | tf_op jit(solution)/shard_map/all_gather | solution.py:176
  9.3 64.1 %all-gather.18.cloned.1.call-start = ((), (), s32[]{:S(2)}) async-start(), calls=%async_computation.7 | async-start | bytes 2359296 | tf_op jit(solution)/shard_map/all_gather | solution.py:194
  10.1 110.6 %all-gather.10.cloned.1.call-start = ((), (), s32[]{:S(2)}) async-start(), calls=%async_computation.3 | async-start | bytes 7077888 | tf_op jit(solution)/shard_map/all_gather | solution.py:174
  10.8 157.0 %all-gather.14.cloned.1.call-start = ((), (), s32[]{:S(2)}) async-start(), calls=%async_computation.5 | async-start | bytes 2359296 | tf_op jit(solution)/shard_map/all_gather | solution.py:175
  11.4 186.1 %all-gather.16.cloned.1.call-start = ((), (), s32[]{:S(2)}) async-start(), calls=%async_computation.6 | async-start | bytes 7077888 | tf_op jit(solution)/shard_map/all_gather | solution.py:192
  12.0 240.0 %all-gather.20.cloned.1.call-start = ((), (), s32[]{:S(2)}) async-start(), calls=%async_computation.8 | async-start | bytes 2359296 | tf_op jit(solution)/shard_map/all_gather | solution.py:193
  12.5 270.6 %all-gather.22.cloned.1.call-start = ((), (), s32[]{:S(2)}) async-start(), calls=%async_computation.9 | async-start | bytes 9437184 | tf_op jit(solution)/shard_map/all_gather | solution.py:215
  13.3 299.9 %all-gather.24.cloned.1.call-start = ((), (), s32[]{:S(2)}) async-start(), calls=%async_computation.10 | async-start | bytes 2359296 | tf_op jit(solution)/shard_map/all_gather | solution.py:218
  14.0 355.3 %all-gather.26.cloned.1.call-start = ((), (), s32[]{:S(2)}) async-start(), calls=%async_computation.11 | async-start | bytes 9437184 | tf_op jit(solution)/shard_map/all_gather | solution.py:216
  16.1 240.6 %copy-start.68 = (f32[1,1024]{1,0:T(1,128)}, f32[1,1024]{1,0:T(1,128)S(1)}, u32[]{:S(2)}) copy-start(f32[1,1024]{1,0:T(1,128)S(1)} %get-tuple-element.41) | copy-start | bytes 12292
  29.0 356.4 %copy-start.40 = (bf16[2,8,16,1024]{3,2,1,0:T(8,128)(2,1)}, bf16[2,8,16,1024]{3,2,1,0:T(8,128)(2,1)S(1)}, u32[]{:S(2)}) copy-start(bf16[2,8,16,1024]{3,2,1,0:T(8,128)(2,1)S(1)} %all_gather.50) | copy-start | bytes 1572868
  43.9 128.6 %copy-start.38 = (bf16[4,2,16,1024]{3,2,1,0:T(8,128)(2,1)}, bf16[4,2,16,1024]{3,2,1,0:T(8,128)(2,1)S(1)}, u32[]{:S(2)}) copy-start(bf16[4,2,16,1024]{3,2,1,0:T(8,128)(2,1)S(1)} %dynamic-slice_bitcast_fusion.1) | copy-start | bytes 786436
  46.3 79.2 %copy-start.45 = (bf16[16,1024]{1,0:T(8,128)(2,1)}, bf16[16,1024]{1,0:T(8,128)(2,1)S(1)}, u32[]{:S(2)}) copy-start(bf16[16,1024]{1,0:T(8,128)(2,1)S(1)} %fusion.77) | copy-start | bytes 98308
  48.5 81.3 %copy-start.47 = (bf16[16,1024]{1,0:T(8,128)(2,1)}, bf16[16,1024]{1,0:T(8,128)(2,1)S(1)}, u32[]{:S(2)}) copy-start(bf16[16,1024]{1,0:T(8,128)(2,1)S(1)} %fusion.74) | copy-start | bytes 98308
  49.2 85.2 %copy-start.49 = (bf16[16,1024]{1,0:T(8,128)(2,1)}, bf16[16,1024]{1,0:T(8,128)(2,1)S(1)}, u32[]{:S(2)}) copy-start(bf16[16,1024]{1,0:T(8,128)(2,1)S(1)} %fusion.71) | copy-start | bytes 98308
  74.4 182.3 %copy-start.36 = (bf16[4,2,16,1024]{3,2,1,0:T(8,128)(2,1)}, bf16[4,2,16,1024]{3,2,1,0:T(8,128)(2,1)S(1)}, u32[]{:S(2)}) copy-start(bf16[4,2,16,1024]{3,2,1,0:T(8,128)(2,1)S(1)} %dynamic-slice_bitcast_fusion) | copy-start | bytes 786436
  75.0 132.9 %copy-start.41 = (bf16[16,1024]{1,0:T(8,128)(2,1)}, bf16[16,1024]{1,0:T(8,128)(2,1)S(1)}, u32[]{:S(2)}) copy-start(bf16[16,1024]{1,0:T(8,128)(2,1)S(1)} %fusion.92) | copy-start | bytes 98308
  75.7 136.7 %copy-start.43 = (bf16[16,1024]{1,0:T(8,128)(2,1)}, bf16[16,1024]{1,0:T(8,128)(2,1)S(1)}, u32[]{:S(2)}) copy-start(bf16[16,1024]{1,0:T(8,128)(2,1)S(1)} %fusion.89) | copy-start | bytes 98308
  173.7 83.1 %copy-start.59 = (f32[1024]{0:T(1024)}, f32[1024]{0:T(1024)S(1)}, u32[]{:S(2)}) copy-start(f32[1024]{0:T(1024)S(1)} %broadcast_multiply_fusion.2) | copy-start | bytes 12292
  174.2 82.5 %copy-start.66 = (f32[1024]{0:T(1024)}, f32[1024]{0:T(1024)S(1)}, u32[]{:S(2)}) copy-start(f32[1024]{0:T(1024)S(1)} %fusion.141) | copy-start | bytes 12292
  611.8 47.4 %all-to-all-start.1 = ((bf16[8,2,2048]{2,1,0:T(2,128)(2,1)}), bf16[8,2,2048]{2,1,0:T(2,128)(2,1)S(1)}, u32[]{:S(2)}, u32[]{:S(2)}) async-start(bf16[8,2,2048]{2,1,0:T(2,128)(2,1)} %reshape.240), calls=%async_computation.1 | async-start | bytes 131072 | tf_op jit(solution)/shard_map/all_to_all | solution.py:349
  659.2 11.2 %all-to-all-start.2 = ((bf16[8,2,8192]{2,1,0:T(2,128)(2,1)}), bf16[8,2,8192]{2,1,0:T(2,128)(2,1)}, u32[]{:S(2)}, u32[]{:S(2)}) async-start(bf16[8,2,8192]{2,1,0:T(2,128)(2,1)} %reshape.242), calls=%async_computation.2 | async-start | bytes 524288 | tf_op jit(solution)/shard_map/all_to_all | solution.py:356
  670.3 18.2 %all-to-all-start = ((bf16[8,2,16384]{2,1,0:T(2,128)(2,1)}), bf16[8,2,16384]{2,1,0:T(2,128)(2,1)S(1)}, u32[]{:S(2)}, u32[]{:S(2)}) async-start(bf16[8,2,16384]{2,1,0:T(2,128)(2,1)} %reshape.238), calls=%async_computation | async-start | bytes 1048576 | tf_op jit(solution)/shard_map/all_to_all | solution.py:342
  673.8 79.5 %all-reduce.4.cloned.1.call-start = ((), (), s32[]{:S(2)}) async-start(), calls=%async_computation.12 | async-start | bytes 1703936 | tf_op jit(solution)/shard_map/psum | solution.py:372
  (74 other events, 523.6 us)
Sparse Core Ops, SparseCore 0:
  10.5 32.2 all-gather.11
  45.2 28.0 all-gather.17
  75.3 45.3 all-gather.9
  122.4 27.7 all-gather.13
  152.0 45.3 all-gather.15
  199.2 27.7 all-gather.19
  228.9 54.2 all-gather.21
  285.0 28.0 all-gather.23
  315.1 54.2 all-gather.25
  706.2 47.1 all-reduce.3

commit v2 on v1

--- a/solution.py
+++ b/solution.py
@@ -148,6 +148,62 @@
         name="attn_bwd_%s_%d_%s"%("m" if masked else "f",tq,mode))(prefix,q,k,v,do,lse)
 
 
+def select_kernel(ids_ref, att_ref, nar_ref, wide_ref, thin_out, wide_out):
+    thin_out[0, :16] = att_ref[:, 0]
+    thin_out[0, 16:] = nar_ref[:, 0]
+    wide_out[0] = wide_ref[:, 0]
+
+
+def select_rows(group_ids, attention_adapters, narrow_adapters, wide_adapters):
+    count = group_ids.shape[0]
+    slots, rank, width = attention_adapters.shape[2:]
+    wide = wide_adapters.shape[3]
+    flat = attention_adapters.reshape(16, slots, rank, width)
+    pick = lambda dest, ids: (0, ids[dest], 0, 0)
+    place = lambda dest, ids: (dest, 0, 0, 0)
+    return pl.pallas_call(
+        select_kernel,
+        grid_spec=pltpu.PrefetchScalarGridSpec(
+            num_scalar_prefetch=1,
+            grid=(count,),
+            in_specs=[
+                pl.BlockSpec((16, 1, rank, width), pick),
+                pl.BlockSpec((2, 1, rank, width), pick),
+                pl.BlockSpec((2, 1, rank, wide), pick),
+            ],
+            out_specs=[
+                pl.BlockSpec((1, 18, rank, width), place),
+                pl.BlockSpec((1, 2, rank, wide), place),
+            ],
+        ),
+        out_shape=[
+            jax.ShapeDtypeStruct((count, 18, rank, width), jnp.bfloat16),
+            jax.ShapeDtypeStruct((count, 2, rank, wide), jnp.bfloat16),
+        ],
+        name="select_rows",
+    )(group_ids, flat, narrow_adapters, wide_adapters)
+
+
+def exchange(rows):
+    return lax.all_to_all(rows, "shard", split_axis=0, concat_axis=0, tiled=True)
+
+
+def join_columns(pieces):
+    count, blocks, rank, width = pieces.shape
+    return pieces.transpose(1, 2, 0, 3).reshape(blocks, rank, count * width)
+
+
+def split_columns(parts, count):
+    stack = jnp.stack(parts).astype(jnp.bfloat16)
+    blocks, rank, width = stack.shape
+    return stack.reshape(blocks, rank, count, width // count).transpose(2, 0, 1, 3)
+
+
+def sum_slots(received, selector):
+    picked = selector[:, None, :, None, None] * received.astype(jnp.float32)[:, :, None]
+    return jnp.sum(picked, axis=0).astype(jnp.bfloat16)
+
+
 def on_device(
     hidden_in,
     enc_states,
@@ -169,13 +225,26 @@
     hidden = hidden_in[0]
     encoder = enc_states[0]
     upstream = cotangent[0].astype(jnp.float32)
-    adapter_slot = adapter_ids[0]
-    self_full, self_out_full, self_adapt = (
-        lax.all_gather(self_qkv, "shard", axis=1, tiled=True),
-        lax.all_gather(self_out, "shard", axis=0, tiled=True),
-        lax.all_gather(attention_adapters[:4], "shard", axis=4, tiled=True),
-    )
-    self_sel = lax.dynamic_index_in_dim(self_adapt, adapter_slot, 2, keepdims=False)
+    slot_count = attention_adapters.shape[2]
+    self_full = lax.all_gather(self_qkv, "shard", axis=1, tiled=True)
+    group_ids = lax.all_gather(adapter_ids, "shard", axis=0, tiled=True)
+    group_size = group_ids.shape[0]
+    thin_pick, wide_pick = select_rows(
+        group_ids, attention_adapters, narrow_adapters, wide_adapters
+    )
+    thin_rows = join_columns(exchange(thin_pick))
+    wide_rows = join_columns(exchange(wide_pick))
+    middle = jnp.concatenate([cross_qkv, self_out[None], cross_out[None]], axis=0)
+    middle_full = lax.all_gather(middle, "shard", axis=1, tiled=True)
+    cross_full = middle_full[:3]
+    self_out_full = middle_full[3]
+    cross_out_full = middle_full[4]
+    expand_full = lax.all_gather(expand_weight, "shard", axis=0, tiled=True)
+    reduce_full = lax.all_gather(reduce_weight, "shard", axis=0, tiled=True)
+    self_sel = thin_rows[:8].reshape(4, 2, *thin_rows.shape[1:])
+    cross_sel = thin_rows[8:16].reshape(4, 2, *thin_rows.shape[1:])
+    narrow_sel = thin_rows[16:]
+    wide_sel = wide_rows
     query_f, query_red = project_forward(hidden, self_full[0], self_sel[0, 0], self_sel[0, 1])
     key_f, key_red = project_forward(hidden, self_full[1], self_sel[1, 0], self_sel[1, 1])
     value_f, value_red = project_forward(hidden, self_full[2], self_sel[2, 0], self_sel[2, 1])
@@ -188,12 +257,6 @@
     )
     self_sum = hidden.astype(jnp.float32) + self_branch
     after_self = layer_norm(self_sum, norm_gains[0], norm_shifts[0])
-    cross_full, cross_out_full, cross_adapt = (
-        lax.all_gather(cross_qkv, "shard", axis=1, tiled=True),
-        lax.all_gather(cross_out, "shard", axis=0, tiled=True),
-        lax.all_gather(attention_adapters[4:], "shard", axis=4, tiled=True),
-    )
-    cross_sel = lax.dynamic_index_in_dim(cross_adapt, adapter_slot, 2, keepdims=False)
     cross_in = after_self.astype(jnp.bfloat16)
     cquery_f, cquery_red = project_forward(
         cross_in, cross_full[0], cross_sel[0, 0], cross_sel[0, 1]
@@ -211,14 +274,6 @@
     )
     cross_sum = after_self + cross_branch
     after_cross = layer_norm(cross_sum, norm_gains[1], norm_shifts[1])
-    expand_full, reduce_full, narrow_full, wide_full = (
-        lax.all_gather(expand_weight, "shard", axis=0, tiled=True),
-        lax.all_gather(reduce_weight, "shard", axis=0, tiled=True),
-        lax.all_gather(narrow_adapters, "shard", axis=3, tiled=True),
-        lax.all_gather(wide_adapters, "shard", axis=3, tiled=True),
-    )
-    narrow_sel = lax.dynamic_index_in_dim(narrow_full, adapter_slot, 1, keepdims=False)
-    wide_sel = lax.dynamic_index_in_dim(wide_full, adapter_slot, 1, keepdims=False)
     feed_in = after_cross.astype(jnp.bfloat16)
     expanded, expand_red = project_forward(feed_in, expand_full, narrow_sel[0], wide_sel[0])
     cdf = 0.5 + 0.5 * lax.erf(expanded * 0.7071067811865476)
@@ -227,152 +282,125 @@
     feed_branch, reduce_red = project_forward(active, reduce_full, wide_sel[1], narrow_sel[1])
     feed_sum = after_cross + feed_branch
     layer_out = layer_norm(feed_sum, norm_gains[2], norm_shifts[2]).astype(jnp.bfloat16)
-    expand_reverse, reduce_back, narrow_back, wide_back = (
-        lax.all_gather(expand_weight, "shard", axis=0, tiled=True),
-        lax.all_gather(reduce_weight, "shard", axis=0, tiled=True),
-        lax.all_gather(narrow_adapters, "shard", axis=3, tiled=True),
-        lax.all_gather(wide_adapters, "shard", axis=3, tiled=True),
-    )
-    narrow_bsel = lax.dynamic_index_in_dim(narrow_back, adapter_slot, 1, keepdims=False)
-    wide_bsel = lax.dynamic_index_in_dim(wide_back, adapter_slot, 1, keepdims=False)
     grad_feed = norm_backward(feed_sum, norm_gains[2], norm_shifts[2], upstream)
     active_grad, reduce_down_grad, reduce_up_gradient = projection_backward(
         grad_feed.astype(jnp.bfloat16),
         active,
         reduce_red,
-        reduce_back,
-        wide_bsel[1],
-        narrow_bsel[1],
+        reduce_full,
+        wide_sel[1],
+        narrow_sel[1],
     )
     expanded_grad = (active_grad.astype(jnp.bfloat16).astype(jnp.float32) * slope).astype(
         jnp.bfloat16
     )
     feed_in_grad, expand_down_grad, expand_up_grad = projection_backward(
-        expanded_grad, feed_in, expand_red, expand_reverse, narrow_bsel[0], wide_bsel[0]
+        expanded_grad, feed_in, expand_red, expand_full, narrow_sel[0], wide_sel[0]
     )
     after_cross_grad = grad_feed + feed_in_grad
-    cross_back, cross_out_back, cross_adapt_back = (
-        lax.all_gather(cross_qkv, "shard", axis=1, tiled=True),
-        lax.all_gather(cross_out, "shard", axis=0, tiled=True),
-        lax.all_gather(attention_adapters[4:], "shard", axis=4, tiled=True),
-    )
-    cross_bsel = lax.dynamic_index_in_dim(cross_adapt_back, adapter_slot, 2, keepdims=False)
     grad_cross = norm_backward(cross_sum, norm_gains[1], norm_shifts[1], after_cross_grad)
     cross_mixed_grad, cout_down, cout_up = projection_backward(
         grad_cross.astype(jnp.bfloat16),
         cross_mixed,
         cross_out_red,
-        cross_out_back,
-        cross_bsel[3, 0],
-        cross_bsel[3, 1],
-    )
+        cross_out_full,
+        cross_sel[3, 0],
+        cross_sel[3, 1],
+    )
+    selector = (
+        group_ids[:, None] == jnp.arange(slot_count, dtype=jnp.int32)[None, :]
+    ).astype(jnp.float32)
+    feed_send = [cout_down, cout_up, expand_down_grad, reduce_up_gradient]
+    feed_thin = exchange(split_columns(feed_send, group_size))
+    feed_wide = exchange(split_columns([expand_up_grad, reduce_down_grad], group_size))
+    feed_parts = (sum_slots(feed_thin, selector), sum_slots(feed_wide, selector))
+    cross_mixed_low, feed_parts = lax.optimization_barrier(
+        (cross_mixed_grad.astype(jnp.bfloat16), feed_parts)
+    )
+    feed_sums = lax.psum(feed_parts, "rep")
     cquery_grad, ckey_grad, cvalue_grad = attn_bwd(
         cross_queries,
         cross_keys,
         cross_values,
-        cross_mixed_grad.astype(jnp.bfloat16),
+        cross_mixed_low,
         cross_lse,
         prefix_len,
         False,
     )
+    cquery_grad, ckey_grad, cvalue_grad, feed_sums = lax.optimization_barrier(
+        (cquery_grad, ckey_grad, cvalue_grad, feed_sums)
+    )
     cross_in_grad, cquery_down, cquery_up = projection_backward(
-        cquery_grad, cross_in, cquery_red, cross_back[0], cross_bsel[0, 0], cross_bsel[0, 1]
+        cquery_grad, cross_in, cquery_red, cross_full[0], cross_sel[0, 0], cross_sel[0, 1]
     )
     enc_key_grad, ckey_down, ckey_up = projection_backward(
-        ckey_grad, encoder, ckey_red, cross_back[1], cross_bsel[1, 0], cross_bsel[1, 1]
+        ckey_grad, encoder, ckey_red, cross_full[1], cross_sel[1, 0], cross_sel[1, 1]
     )
     enc_value_grad, cvalue_down, cvalue_up = projection_backward(
-        cvalue_grad, encoder, cvalue_red, cross_back[2], cross_bsel[2, 0], cross_bsel[2, 1]
+        cvalue_grad, encoder, cvalue_red, cross_full[2], cross_sel[2, 0], cross_sel[2, 1]
     )
     encoder_grad = enc_key_grad + enc_value_grad
     after_self_grad = grad_cross + cross_in_grad
-    self_back, self_out_back, self_adapt_back = (
-        lax.all_gather(self_qkv, "shard", axis=1, tiled=True),
-        lax.all_gather(self_out, "shard", axis=0, tiled=True),
-        lax.all_gather(attention_adapters[:4], "shard", axis=4, tiled=True),
-    )
-    self_bsel = lax.dynamic_index_in_dim(self_adapt_back, adapter_slot, 2, keepdims=False)
     grad_self = norm_backward(self_sum, norm_gains[0], norm_shifts[0], after_self_grad)
     self_mixed_grad, sout_down, sout_up = projection_backward(
         grad_self.astype(jnp.bfloat16),
         self_mixed,
         self_out_red,
-        self_out_back,
-        self_bsel[3, 0],
-        self_bsel[3, 1],
-    )
+        self_out_full,
+        self_sel[3, 0],
+        self_sel[3, 1],
+    )
+    cross_send = [
+        sout_down,
+        sout_up,
+        cquery_down,
+        cquery_up,
+        ckey_down,
+        ckey_up,
+        cvalue_down,
+        cvalue_up,
+    ]
+    cross_part = sum_slots(exchange(split_columns(cross_send, group_size)), selector)
+    self_mixed_low, cross_part, encoder_grad = lax.optimization_barrier(
+        (self_mixed_grad.astype(jnp.bfloat16), cross_part, encoder_grad)
+    )
+    cross_sum_rep = lax.psum(cross_part, "rep")
     query_grad, key_grad, value_grad = attn_bwd(
         queries,
         keys_in,
         values_in,
-        self_mixed_grad.astype(jnp.bfloat16),
+        self_mixed_low,
         self_lse,
         prefix_len,
         True,
     )
+    query_grad, key_grad, value_grad, cross_sum_rep = lax.optimization_barrier(
+        (query_grad, key_grad, value_grad, cross_sum_rep)
+    )
     hid_query, squery_down, squery_up = projection_backward(
-        query_grad, hidden, query_red, self_back[0], self_bsel[0, 0], self_bsel[0, 1]
+        query_grad, hidden, query_red, self_full[0], self_sel[0, 0], self_sel[0, 1]
     )
     hidden_key_rows, self_key_down, self_key_up = projection_backward(
-        key_grad, hidden, key_red, self_back[1], self_bsel[1, 0], self_bsel[1, 1]
+        key_grad, hidden, key_red, self_full[1], self_sel[1, 0], self_sel[1, 1]
     )
     hid_value, svalue_down, svalue_up = projection_backward(
-        value_grad, hidden, value_red, self_back[2], self_bsel[2, 0], self_bsel[2, 1]
+        value_grad, hidden, value_red, self_full[2], self_sel[2, 0], self_sel[2, 1]
     )
     hidden_grad = grad_self + hid_query + hidden_key_rows + hid_value
-    attention_parts = (
-        (squery_down, squery_up),
-        (self_key_down, self_key_up),
-        (svalue_down, svalue_up),
-        (sout_down, sout_up),
-        (cquery_down, cquery_up),
-        (ckey_down, ckey_up),
-        (cvalue_down, cvalue_up),
-        (cout_down, cout_up),
-    )
-    attention_stack = jnp.stack(
-        [jnp.stack([down_part, up_part]) for down_part, up_part in attention_parts]
-    )
-    narrow_stack = jnp.stack([expand_down_grad, reduce_up_gradient])
-    wide_stack = jnp.stack([expand_up_grad, reduce_down_grad])
-    adapter_slot_count = attention_adapters.shape[2]
-    rank_rows = attention_stack.shape[2]
-    attention_fragment = attention_stack.reshape(1, 16, rank_rows, attention_stack.shape[3])
-    received = (
-        lax.all_to_all(
-            attention_fragment.astype(jnp.bfloat16),
-            "shard",
-            split_axis=3,
-            concat_axis=0,
-            tiled=True,
-        ).astype(attention_fragment.dtype),
-        lax.all_to_all(
-            narrow_stack[None].astype(jnp.bfloat16),
-            "shard",
-            split_axis=3,
-            concat_axis=0,
-            tiled=True,
-        ).astype(jnp.float32),
-        lax.all_to_all(
-            wide_stack[None].astype(jnp.bfloat16), "shard", split_axis=3, concat_axis=0, tiled=True
-        ).astype(jnp.float32),
-    )
-    group_ids = lax.all_gather(adapter_ids, "shard", axis=0, tiled=True)
-    one_hot = (
-        group_ids[:, None] == jnp.arange(adapter_slot_count, dtype=jnp.int32)[None, :]
-    ).astype(jnp.float32)
-    selector = one_hot[:, None, :, None, None]
-    owned_attention = jnp.sum(selector * received[0][:, :, None], axis=0)
-    owned_attention = owned_attention.reshape(
-        8, 2, adapter_slot_count, rank_rows, owned_attention.shape[3]
-    )
-    owned_narrow = jnp.sum(selector * received[1][:, :, None], axis=0)
-    owned_wide = jnp.sum(selector * received[2][:, :, None], axis=0)
-    attention_grad, narrow_grad, wide_grad = (
-        lax.psum(owned_attention.astype(jnp.bfloat16), "rep").astype(jnp.float32),
-        lax.psum(owned_narrow.astype(jnp.bfloat16), "rep").astype(jnp.float32),
-        lax.psum(owned_wide.astype(jnp.bfloat16), "rep").astype(jnp.float32),
-    )
+    late_thin = exchange(
+        split_columns(
+            [squery_down, squery_up, self_key_down, self_key_up, svalue_down, svalue_up],
+            group_size,
+        )
+    )
+    late_sum = lax.psum(sum_slots(late_thin, selector), "rep")
+    attention_grad = (
+        jnp.concatenate([late_sum, cross_sum_rep, feed_sums[0][:2]], axis=0)
+        .astype(jnp.float32)
+        .reshape(attention_adapters.shape)
+    )
+    narrow_grad = feed_sums[0][2:].astype(jnp.float32)
+    wide_grad = feed_sums[1].astype(jnp.float32)
     return (
         layer_out[None],
         hidden_grad[None],

time: 776 us -> 589 us (0.76)
  waiting for transfers between devices: 211 us -> 72.3 us
  local copies, waits for them, and re-layouts: 58.3 us -> 24.7 us
  other arithmetic: 38.6 us -> 24.2 us
  starting transfers between devices: 11.6 us -> 22.7 us
  blocking collectives: 20.1 us -> 9.99 us
    all_gather x9 -> x4, waiting for transfers between devices: 167 us -> 24.6 us  [the longest x1 15.4 us: on_device(): reduce_full = lax.all_gather(reduce_weight, 'shard', axis=0, tiled=True)]
    unnamed x179 -> x207, local copies, waits for them, and re-layouts: 34.3 us -> 14.7 us
    all_to_all x3 -> x6, waiting for transfers between devices: 3.23 us -> 20.4 us  [exchange(): lax.all_to_all(rows, 'shard', split_axis=0, concat_axis=0, tiled=True)]
    convert_element_type x4 -> x0, local copies, waits for them, and re-layouts: 15.7 us -> none  [the longest x3 11 us: on_device(): received = (lax.all_to_all(attention_fragment.astype(jnp.bfloat16), 'shar...]
    convert_element_type x7 -> x8, other arithmetic: 18.8 us -> 4.05 us  [the longest x1 1.31 us: on_device(): selector = (group_ids[:, None] == jnp.arange(slot_count, dtype=jnp.int32)...]
    all_gather x1 -> x0, blocking collectives: 12.9 us -> none  [on_device(): lax.all_gather(narrow_adapters, 'shard', axis=3, tiled=True)]
    psum x1 -> x3, waiting for transfers between devices: 36.1 us -> 25.4 us  [the longest x1 25.3 us: on_device(): late_sum = lax.psum(sum_slots(late_thin, selector), 'rep')]
    all_to_all x3 -> x6, starting transfers between devices: 11.2 us -> 21.9 us  [exchange(): lax.all_to_all(rows, 'shard', split_axis=0, concat_axis=0, tiled=True)]
  transfers between devices with their start and end apart: 13 -> 13, of which waited for: 9 -> 6; matrix products, arithmetic and copies ran while one was open for 22% -> 28% of each run, Pallas kernels for 8% -> 30%
where the time goes in v2:
time: 589 us; the launch traced here: 578 us
  matrix products  235 us (40%)
  Pallas kernels  172 us (29%)
  waiting for transfers between devices  72.3 us (12%)
  local copies, waits for them, and re-layouts  24.7 us (4%)
  other arithmetic  24.2 us (4%)
  starting transfers between devices  22.7 us (4%)
  between operations  17.4 us (3%)
  blocking collectives  9.99 us (2%)
    pallas_call x2, Pallas kernels, attn_bwd(): pl.pallas_call(functools.partial(bwd_kernel, masked=masked, tq=tq, mode=m...  103 us
    dot_general x30, matrix products, contract_last(): lax.dot_general(left, right, (((1,), (1,)), ((), ())), preferred_element_...  94.5 us
    pallas_call x2, Pallas kernels, attn_fwd(): pl.pallas_call(functools.partial(fwd_kernel, masked=masked, tq=tq), grid=...  64.2 us
    dot_general x10, matrix products, project_forward(): output = jnp.dot(inputs, weight, preferred_element_type=jnp.float32)  52.3 us
    dot_general x10, matrix products, projection_backward(): jnp.dot(reduced_grad, down_rows, preferred_element_type=jnp.float32)  45.4 us
    dot_general x10, matrix products, project_forward(): jnp.dot(reduced, up_rows, preferred_element_type=jnp.float32)  27.9 us
    psum x1, waiting for transfers between devices, on_device(): late_sum = lax.psum(sum_slots(late_thin, selector), 'rep')  25.3 us
    all_to_all x6, starting transfers between devices, exchange(): lax.all_to_all(rows, 'shard', split_axis=0, concat_axis=0, tiled=True)  21.9 us
  transfers between devices with their start and end apart: 13, of which 6 were waited for; matrix products, arithmetic and copies ran while one was open for 28% of the time, Pallas kernels for 30%

profile of v2, /device:TPU:0, one launch (start us, length us, event | category | flops | bytes accessed | tf_op | source)
XLA Modules:
  0.0 578.4 jit_solution(2082499690986773053)
XLA Ops:
  13.3 10.0 %all-reduce.ids_ref = s32[8]{0:T(128)} all-reduce(s32[8]{0:T(128)S(1)} %dynamic-update-slice), channel_id=1, replica_groups=mesh['shard'=8,'rep'=4] {'shard'}, use_global_device_ids=true, to_apply=%add | all-reduce | flops 8 | bytes 64
  23.3 5.3 select_rows.1
  33.1 5.6 all-to-all-done.1
  46.3 13.2 %all-to-all-done = bf16[8,18,16,128]{3,2,1,0:T(8,128)(2,1)S(1)} async-done(((bf16[8,18,16,128]{3,2,1,0:T(8,128)(2,1)}), bf16[8,18,16,128]{3,2,1,0:T(8,128)(2,1)S(1)}, u32[]{:S(2)}, u32[]{:S(2)}) %all-to-all-start) | async-done | bytes 589856 | tf_op jit(solution)/shard_map/all_to_all | solution.py:188
  89.8 28.8 %attn_fwd_m_256.1 = (bf16[1024,1024]{1,0:T(8,128)(2,1)}, f32[8,1024,2]{2,1,0:T(8,128)}) custom-call(s32[1]{0:T(128)S(6)} %copy.249.prefix_ref, bf16[1024,1024]{1,0:T(8,128)(2,1)} %add_convert_fusion.7.q_ref, bf16[1024,1024]{1,0:T(8,128)(2,1)} %add_convert_fusion.6.k_ref, bf16[1024,1024]{1,0:T(8,128)(2,1)} %add_convert_fusion.5.v_ref), custom_call_target="tpu_custom_call" | custom-call | tf_op jit(solution)/shard_map/attn_fwd_m_256/pallas_call | solution.py:101
  120.9 9.1 %all-gather.7.cloned.1.call-done = bf16[5,1024,1024]{2,1,0:T(8,128)(2,1)} async-done(((bf16[5,128,1024]{2,1,0:T(8,128)(2,1)}), bf16[5,1024,1024]{2,1,0:T(8,128)(2,1)}) %all-gather.7.cloned.1.call-update) | async-done | bytes 10485776 | tf_op jit(solution)/shard_map/all_gather | solution.py:238
  152.0 35.3 %attn_fwd_f_256.1 = (bf16[1024,1024]{1,0:T(8,128)(2,1)}, f32[8,1024,2]{2,1,0:T(8,128)}) custom-call(s32[1]{0:T(128)S(6)} %copy.249.prefix_ref, bf16[1024,1024]{1,0:T(8,128)(2,1)} %add_convert_fusion.4.q_ref, bf16[1024,1024]{1,0:T(8,128)(2,1)} %fusion.11.k_ref, bf16[1024,1024]{1,0:T(8,128)(2,1)} %fusion.10.v_ref), custom_call_target="tpu_custom_call" | custom-call | tf_op jit(solution)/shard_map/attn_fwd_f_256/pallas_call | solution.py:101
  189.6 4.7 fusion.43
  198.5 11.6 %fusion.134 = f32[1024,4096]{1,0:T(8,128)S(1)} fusion(bf16[1024,1024]{1,0:T(8,128)(2,1)S(1)} %fusion.13, bf16[1024,4096]{1,0:T(8,128)(2,1)} %all-gather.9.cloned.1.call-done), kind=kOutput, calls=%fused_computation.249 | convolution fusion | flops 8589934592 | bytes 27262976 | tf_op jit(solution)/shard_map/dot_general | solution.py:44
  210.2 10.2 %multiply_convert_fusion = (bf16[1024,4096]{1,0:T(8,128)(2,1)S(1)}, f32[1024,4096]{1,0:T(8,128)}) fusion(f32[1024,4096]{1,0:T(8,128)S(1)} %fusion.134, bf16[1024,16]{0,1:T(8,128)(2,1)S(1)} %convolution_convert_fusion.11, bf16[16,4096]{1,0:T(8,128)(2,1)} %bitcast.408), kind=kOutput, calls=%fused_computation.8 | convolution fusion | flops 163577856 | bytes 42106880 | tf_op jit(solution)/shard_map/dot_general | solution.py:45
  226.9 15.4 %all-gather.11.cloned.1.call-done = bf16[4096,1024]{1,0:T(8,128)(2,1)} async-done(((bf16[512,1024]{1,0:T(8,128)(2,1)}), bf16[4096,1024]{1,0:T(8,128)(2,1)}) %all-gather.11.cloned.1.call-update) | async-done | bytes 8388624 | tf_op jit(solution)/shard_map/all_gather | solution.py:243
  242.3 12.7 %fusion.135 = f32[1024,1024]{1,0:T(8,128)S(1)} fusion(bf16[1024,4096]{1,0:T(8,128)(2,1)} %copy-done, bf16[4096,1024]{1,0:T(8,128)(2,1)} %all-gather.11.cloned.1.call-done), kind=kOutput, calls=%fused_computation.250 | convolution fusion | flops 8589934592 | bytes 20971520 | tf_op jit(solution)/shard_map/dot_general | solution.py:44
  264.4 14.6 %fusion.136 = f32[1024,4096]{1,0:T(8,128)} fusion(bf16[1024,1024]{1,0:T(8,128)(2,1)S(1)} %add_convert_fusion.10, bf16[4096,1024]{1,0:T(8,128)(2,1)} %all-gather.11.cloned.1.call-done), kind=kOutput, calls=%fused_computation.251 | convolution fusion | flops 8589934592 | bytes 27262976 | tf_op jit(solution)/shard_map/dot_general | solution.py:31
  279.0 14.1 %fusion.5 = bf16[1024,4096]{1,0:T(8,128)(2,1)S(1)} fusion(f32[1024,4096]{1,0:T(8,128)} %get-tuple-element.92, f32[1024,4096]{1,0:T(8,128)} %fusion.136, bf16[1024,16]{0,1:T(8,128)(2,1)S(1)} %fusion.44, bf16[16,4096]{1,0:T(8,128)(2,1)S(1)} %bitcast.412), kind=kOutput, calls=%fused_computation.6 | convolution fusion | flops 188743680 | bytes 42106880 | tf_op jit(solution)/shard_map/dot_general | solution.py:51
  297.0 11.5 %fusion.137 = f32[1024,1024]{1,0:T(8,128)S(1)} fusion(bf16[1024,4096]{1,0:T(8,128)(2,1)S(1)} %fusion.5, bf16[1024,4096]{1,0:T(8,128)(2,1)} %all-gather.9.cloned.1.call-done), kind=kOutput, calls=%fused_computation.252 | convolution fusion | flops 8589934592 | bytes 20971520 | tf_op jit(solution)/shard_map/dot_general | solution.py:31
  319.1 5.9 %fusion.42 = f32[1024,1024]{1,0:T(8,128)} fusion(bf16[1024,1024]{1,0:T(8,128)(2,1)S(1)} %add_convert_fusion.9, bf16[5,1024,1024]{2,1,0:T(8,128)(2,1)} %all-gather.7.cloned.1.call-done), kind=kOutput, calls=%fused_computation.91 | convolution fusion | flops 2147483648 | bytes 8388608 | tf_op jit(solution)/shard_map/dot_general | solution.py:31
  341.0 58.1 %attn_bwd_f_256_wt.1 = (bf16[1024,1024]{1,0:T(8,128)(2,1)}, bf16[1024,1024]{1,0:T(8,128)(2,1)}, bf16[1024,1024]{1,0:T(8,128)(2,1)}) custom-call(s32[1]{0:T(128)S(6)} %copy.249.prefix_ref, bf16[1024,1024]{1,0:T(8,128)(2,1)} %add_convert_fusion.4.q_ref, bf16[1024,1024]{1,0:T(8,128)(2,1)} %fusion.11.k_ref, bf16[1024,1024]{1,0:T(8,128)(2,1)} %fusion.10.v_ref, ...), custom_call_target="tpu_custom_call" | custom-call | tf_op jit(solution)/shard_map/attn_bwd_f_256_wt/pallas_call | solution.py:143
  425.5 4.7 fusion.41
  448.9 44.7 %attn_bwd_m_256_wt.1 = (bf16[1024,1024]{1,0:T(8,128)(2,1)}, bf16[1024,1024]{1,0:T(8,128)(2,1)}, bf16[1024,1024]{1,0:T(8,128)(2,1)}) custom-call(s32[1]{0:T(128)S(6)} %copy.249.prefix_ref, bf16[1024,1024]{1,0:T(8,128)(2,1)} %add_convert_fusion.7.q_ref, bf16[1024,1024]{1,0:T(8,128)(2,1)} %add_convert_fusion.6.k_ref, ...), custom_call_target="tpu_custom_call" | custom-call | tf_op jit(solution)/shard_map/attn_bwd_m_256_wt/pallas_call | solution.py:143
  510.0 6.6 %fusion.35 = f32[1024,1024]{1,0:T(8,128)} fusion(bf16[1024,1024]{1,0:T(8,128)(2,1)} %get-tuple-element.55, bf16[3,1024,1024]{2,1,0:T(8,128)(2,1)} %all-gather.5.cloned.1.call-done), kind=kOutput, calls=%fused_computation.84 | convolution fusion | flops 2147483648 | bytes 8388608 | tf_op jit(solution)/shard_map/dot_general | solution.py:31
  516.6 6.1 %fusion.34 = f32[1024,1024]{1,0:T(8,128)} fusion(bf16[1024,1024]{1,0:T(8,128)(2,1)S(1)} %copy-done.25, bf16[3,1024,1024]{2,1,0:T(8,128)(2,1)} %all-gather.5.cloned.1.call-done), kind=kOutput, calls=%fused_computation.83 | convolution fusion | flops 2147483648 | bytes 8388608 | tf_op jit(solution)/shard_map/dot_general | solution.py:31
  522.7 6.0 %fusion.33 = f32[1024,1024]{1,0:T(8,128)} fusion(bf16[1024,1024]{1,0:T(8,128)(2,1)S(1)} %copy-done.24, bf16[3,1024,1024]{2,1,0:T(8,128)(2,1)} %all-gather.5.cloned.1.call-done), kind=kOutput, calls=%fused_computation.82 | convolution fusion | flops 2147483648 | bytes 8388608 | tf_op jit(solution)/shard_map/dot_general | solution.py:31
  532.5 11.2 %add_bitcast_fusion = f32[1,1024,1024]{2,1,0:T(8,128)} fusion(f32[1024,1024]{1,0:T(8,128)} %fusion.35, f32[1024,1024]{1,0:T(8,128)} %fusion.34, f32[1024,1024]{1,0:T(8,128)} %fusion.111, f32[1024,1024]{1,0:T(8,128)} %fusion.33, f32[1024,1024]{1,0:T(8,128)} %fusion.110, f32[1024,1024]{1,0:T(8,128)} %copy-done.10, bf16[1024,16]{0,1:T(8,128)(2,1)S(1)} %fusion.59, ...), kind=kOutput, calls=%fused_computation.25 | convolution fusion | flops 40894464 | bytes 29429760 | tf_op jit(solution)/shard_map/dot_general | solution.py:51
  543.7 25.3 %all-reduce.8.cloned.1.call-done = bf16[6,8,16,128]{3,2,1,0:T(8,128)(2,1)} async-done(((bf16[6,8,16,128]{3,2,1,0:T(8,128)(2,1)}), bf16[6,8,16,128]{3,2,1,0:T(8,128)(2,1)}) %all-reduce.8.cloned.1.call-update) | async-done | bytes 196624 | tf_op jit(solution)/shard_map/psum | solution.py:396
  (365 shorter events, 190.4 us)
Async XLA Ops:
  7.2 65.9 %all-gather.5.cloned.1.call-start = ((), (), s32[]{:S(2)}) async-start(), calls=%async_computation.6 | async-start | bytes 7077888 | tf_op jit(solution)/shard_map/all_gather | solution.py:229
  7.9 122.1 %all-gather.7.cloned.1.call-start = ((), (), s32[]{:S(2)}) async-start(), calls=%async_computation.7 | async-start | bytes 11796480 | tf_op jit(solution)/shard_map/all_gather | solution.py:238
  8.0 36.3 %copy-start.82 = (f32[3,1024]{1,0:T(4,128)S(1)}, f32[3,1024]{1,0:T(4,128)}, u32[]{:S(2)}) copy-start(f32[3,1024]{1,0:T(4,128)} %param.31) | copy-start | bytes 36868
  10.5 188.0 %all-gather.9.cloned.1.call-start = ((), (), s32[]{:S(2)}) async-start(), calls=%async_computation.8 | async-start | bytes 9437184 | tf_op jit(solution)/shard_map/all_gather | solution.py:242
  28.5 10.3 %all-to-all-start.1 = ((bf16[8,2,16,512]{3,2,1,0:T(8,128)(2,1)}), bf16[8,2,16,512]{3,2,1,0:T(8,128)(2,1)S(1)}, u32[]{:S(2)}, u32[]{:S(2)}) async-start(bf16[8,2,16,512]{3,2,1,0:T(8,128)(2,1)} %get-tuple-element.36), calls=%async_computation.1 | async-start | bytes 524288 | tf_op jit(solution)/shard_map/all_to_all | solution.py:188
  31.9 210.4 %all-gather.11.cloned.1.call-start = ((), (), s32[]{:S(2)}) async-start(), calls=%async_computation.9 | async-start | bytes 9437184 | tf_op jit(solution)/shard_map/all_gather | solution.py:243
  38.8 20.6 %all-to-all-start = ((bf16[8,18,16,128]{3,2,1,0:T(8,128)(2,1)}), bf16[8,18,16,128]{3,2,1,0:T(8,128)(2,1)S(1)}, u32[]{:S(2)}, u32[]{:S(2)}) async-start(bf16[8,18,16,128]{3,2,1,0:T(8,128)(2,1)} %get-tuple-element.33), calls=%async_computation | async-start | bytes 1179648 | tf_op jit(solution)/shard_map/all_to_all | solution.py:188
  60.5 133.8 %copy-start.30 = (bf16[4,2,16,1024]{3,2,1,0:T(8,128)(2,1)}, bf16[4,2,16,1024]{3,2,1,0:T(8,128)(2,1)S(1)}, u32[]{:S(2)}) copy-start(bf16[4,2,16,1024]{3,2,1,0:T(8,128)(2,1)S(1)} %reshape.230) | copy-start | bytes 786436
  65.5 69.2 %copy-start.32 = (bf16[4,2,16,1024]{3,2,1,0:T(8,128)(2,1)}, bf16[4,2,16,1024]{3,2,1,0:T(8,128)(2,1)S(1)}, u32[]{:S(2)}) copy-start(bf16[4,2,16,1024]{3,2,1,0:T(8,128)(2,1)S(1)} %reshape.229) | copy-start | bytes 786436
  73.1 124.8 %copy-start.54 = (bf16[1,16,8,128]{3,2,1,0:T(8,128)(2,1)}, bf16[1,16,8,128]{3,2,1,0:T(8,128)(2,1)S(1)}, u32[]{:S(2)}) copy-start(bf16[1,16,8,128]{3,2,1,0:T(8,128)(2,1)S(1)} %copy.136) | copy-start | bytes 98308
  135.8 58.5 %copy-start.58 = (f32[1024]{0:T(1024)}, f32[1024]{0:T(1024)S(1)}, u32[]{:S(2)}) copy-start(f32[1024]{0:T(1024)S(1)} %broadcast_multiply_fusion.2) | copy-start | bytes 12292
  136.4 57.9 %copy-start.64 = (f32[1024]{0:T(1024)}, f32[1024]{0:T(1024)S(1)}, u32[]{:S(2)}) copy-start(f32[1024]{0:T(1024)S(1)} %fusion.120) | copy-start | bytes 12292
  226.8 28.2 %copy-start.67 = (f32[1024]{0:T(1024)S(1)}, f32[1024]{0:T(1024)}, u32[]{:S(2)}) copy-start(f32[1024]{0:T(1024)} %copy-done.66) | copy-start | bytes 12292
  226.8 28.2 %copy-start.71 = (f32[1,1024]{1,0:T(1,128)S(1)}, f32[1,1024]{1,0:T(1,128)}, u32[]{:S(2)}) copy-start(f32[1,1024]{1,0:T(1,128)} %get-tuple-element.81) | copy-start | bytes 12292
  315.8 10.0 %all-to-all-start.2 = ((bf16[8,4,16,128]{3,2,1,0:T(8,128)(2,1)}), bf16[8,4,16,128]{3,2,1,0:T(8,128)(2,1)S(1)}, u32[]{:S(2)}, u32[]{:S(2)}) async-start(bf16[8,4,16,128]{3,2,1,0:T(8,128)(2,1)} %maximum_bitcast_fusion.1), calls=%async_computation.2 | async-start | bytes 262144 | tf_op jit(solution)/shard_map/all_to_all | solution.py:188
  325.8 11.0 %all-to-all-start.3 = ((bf16[8,2,16,512]{3,2,1,0:T(8,128)(2,1)}), bf16[8,2,16,512]{3,2,1,0:T(8,128)(2,1)S(1)}, u32[]{:S(2)}, u32[]{:S(2)}) async-start(bf16[8,2,16,512]{3,2,1,0:T(8,128)(2,1)} %maximum_bitcast_fusion), calls=%async_computation.3 | async-start | bytes 524288 | tf_op jit(solution)/shard_map/all_to_all | solution.py:188
  329.9 69.2 %all-reduce.10.cloned.1.call-start = ((), (), s32[]{:S(2)}) async-start(), calls=%async_computation.12 | async-start | bytes 786432 | tf_op jit(solution)/shard_map/psum | solution.py:320
  341.0 58.1 %copy-start.51 = (bf16[1024,16]{0,1:T(8,128)(2,1)S(1)}, bf16[1024,16]{0,1:T(8,128)(2,1)}, u32[]{:S(2)}) copy-start(bf16[1024,16]{0,1:T(8,128)(2,1)} %copy-done.50) | copy-start | bytes 98308
  421.9 21.4 %all-to-all-start.4 = ((bf16[8,8,16,128]{3,2,1,0:T(8,128)(2,1)}), bf16[8,8,16,128]{3,2,1,0:T(8,128)(2,1)S(1)}, u32[]{:S(2)}, u32[]{:S(2)}) async-start(bf16[8,8,16,128]{3,2,1,0:T(8,128)(2,1)} %copy.160), calls=%async_computation.4 | async-start | bytes 524288 | tf_op jit(solution)/shard_map/all_to_all | solution.py:188
  425.3 68.3 %all-reduce.6.cloned.1.call-start = ((), (), s32[]{:S(2)}) async-start(), calls=%async_computation.10 | async-start | bytes 524288 | tf_op jit(solution)/shard_map/psum | solution.py:367
  448.9 44.7 %copy-start.43 = (bf16[16,1024]{1,0:T(8,128)(2,1)S(1)}, bf16[16,1024]{1,0:T(8,128)(2,1)}, u32[]{:S(2)}) copy-start(bf16[16,1024]{1,0:T(8,128)(2,1)} %copy-done.42) | copy-start | bytes 98308
  505.6 25.8 %all-to-all-start.5 = ((bf16[8,6,16,128]{3,2,1,0:T(8,128)(2,1)}), bf16[8,6,16,128]{3,2,1,0:T(8,128)(2,1)S(1)}, u32[]{:S(2)}, u32[]{:S(2)}) async-start(bf16[8,6,16,128]{3,2,1,0:T(8,128)(2,1)} %copy.167), calls=%async_computation.5 | async-start | bytes 393216 | tf_op jit(solution)/shard_map/all_to_all | solution.py:188
  509.7 59.3 %all-reduce.8.cloned.1.call-start = ((), (), s32[]{:S(2)}) async-start(), calls=%async_computation.11 | async-start | bytes 393216 | tf_op jit(solution)/shard_map/psum | solution.py:396
  532.5 36.5 %copy-start.57 = (bf16[8,8,16,128]{3,2,1,0:T(8,128)(2,1)S(1)}, bf16[8,8,16,128]{3,2,1,0:T(8,128)(2,1)}, u32[]{:S(2)}) copy-start(bf16[8,8,16,128]{3,2,1,0:T(8,128)(2,1)} %all-reduce.6.cloned.1.call-done) | copy-start | bytes 786436
  (79 other events, 455.7 us)
Sparse Core Ops, SparseCore 0:
  9.9 54.4 all-gather.4
  66.8 63.1 all-gather.6
  131.9 54.2 all-gather.8
  187.9 54.2 all-gather.10
  338.2 36.8 all-reduce.9
  444.6 36.8 all-reduce.5
  532.6 36.3 all-reduce.7
